TPU v7x, 128 devices: a whole 4x4x4 slice. The times are simulated.
128 devices in a mesh: row: 16 (over y, x), col: 8 (over z, core).
Axes of the slice: x: 4, y: 4, z: 4, core: 2. Of those that a mesh axis runs over, the one named last changes fastest.
Arguments:
- snapshots: float32 [65536, 2048], P(('row', 'col')), may hold values from -6 to 6
- district: int32 [65536], P(('row', 'col')), may hold values from 0 to 255, never falling along the last dimension, each value on 1 to 1024 neighbouring positions
- target: int32 [65536], replicated, may hold values from 0 to 65535, as said below
Outputs:
- coefficients: float32 [512, 2048], P(None, 'col')
- remainder: float32 [65536, 2048], P('row', 'col')
Inputs may be any that keep to these rules, and one draw needn't show every extreme that they name: A permutation of the storage rows; each aligned block of 512 nodes has exactly 512 / 16 nodes whose target lies in each aligned block of 4096 storage rows. `district`: districts never fall along the nodes, and each holds at most 1024 nodes.
All inputs are finite; a program needn't handle non-finite values.
Results may differ from a plain program's by a relative error of at most 0.0001.
Values sent between devices are 32-bit elements; how exact they have to be, the bound alone decides.
A program may use at most 128 MiB of HBM per device.

v0:
```python
import jax
import jax.numpy as jnp
from jax import lax
from jax.sharding import PartitionSpec as P

NB = 256
DIST_MEAN = 256


HIGH = lax.Precision.HIGHEST


def from_root(value, axis, source):
    kept = jnp.where(lax.axis_index(axis) == source, value, 0).astype(value.dtype)
    return lax.psum(kept, axis)


def orthonormal(panel, gram):
    lower = jnp.linalg.cholesky(gram)
    inverse = jax.scipy.linalg.solve_triangular(
        lower, jnp.eye(gram.shape[0], dtype=gram.dtype), lower=True
    )
    return jnp.dot(panel, inverse.T, precision=HIGH)


def gram_of(panel):
    return jnp.dot(panel.T, panel, precision=HIGH)


def body(snapshots, district, target):
    n_row = lax.axis_size("row")
    n_col = lax.axis_size("col")
    nodes_dev, snaps = snapshots.shape
    nodes = target.shape[0]
    groups = nodes // DIST_MEAN
    labels = jnp.arange(groups, dtype=jnp.int32)
    member = (district[:, None] == labels[None, :]).astype(jnp.float32)
    counts = lax.psum(jnp.sum(member, axis=0), ("row", "col"))
    scale = jnp.sqrt(DIST_MEAN / jnp.maximum(counts, 1.0))
    weight = jnp.dot(member, scale, precision=HIGH)
    weighted = snapshots * weight[:, None]
    local_rows = nodes // n_row
    per_owner = nodes_dev // n_row
    width = snaps // n_col
    source = lax.axis_index(("row", "col"))
    mine = lax.dynamic_slice_in_dim(target, source * nodes_dev, nodes_dev)
    owner = mine // local_rows
    order = jnp.argsort(owner * nodes_dev + jnp.arange(nodes_dev, dtype=jnp.int32))
    sorted_rows = weighted[order]
    shaped = sorted_rows.reshape(n_row, per_owner, width // NB, n_col, NB)
    shaped = shaped.transpose(0, 3, 1, 2, 4).reshape(n_row, n_col, per_owner, width)
    moved = lax.all_to_all(
        shaped.reshape(n_row * n_col, per_owner, width),
        ("row", "col"),
        split_axis=0,
        concat_axis=0,
        tiled=True,
    )
    arrived = moved.reshape(n_row * n_col * per_owner, width)
    my_row = lax.axis_index("row")
    chosen = jnp.nonzero(target // local_rows == my_row, size=local_rows)[0]
    placing = target[chosen] % local_rows
    inverse = (
        jnp.zeros((local_rows,), jnp.int32).at[placing].set(jnp.arange(local_rows, dtype=jnp.int32))
    )
    block = arrived[inverse]
    stacked = []
    for index in range(2):
        first = index // n_col * NB
        panel = block
        gram = lax.psum(gram_of(panel), "row")
        basis = from_root(orthonormal(panel, gram), "col", index % n_col)
        projection = lax.psum(jnp.dot(basis.T, block, precision=HIGH), "row")
        block = block - jnp.dot(basis, projection, precision=HIGH)
        stacked.append(projection)
    return (jnp.concatenate(stacked, axis=0), block)


def solution(mesh):
    in_specs = (P(("row", "col"), None), P(("row", "col")), P())
    out_specs = (P(None, "col"), P("row", "col"))
    return jax.shard_map(body, mesh=mesh, in_specs=in_specs, out_specs=out_specs, check_vma=False)
```

profile of v0, /device:TPU:1, one launch (start us, length us, event | category | flops | bytes accessed | tf_op | source)
XLA Modules:
  0.0 1310.4 jit_solution(6391460466063920243)
XLA Ops:
  7.2 0.8 fusion.37
  7.9 3.8 sort.17
  11.7 0.8 convert_reduce_fusion
  12.6 68.7 %psum.49 = f32[256]{0:T(256)S(1)} all-reduce(f32[256]{0:T(256)S(1)} %convert_reduce_fusion), channel_id=1, replica_groups=mesh['row'=16,'col'=8] {'row','col'}, use_global_device_ids=true, to_apply=%region_1.0 | all-reduce | flops 256 | bytes 2048 | tf_op jit(solution)/shard_map/psum | solution.py:38
  81.3 1.1 fusion
  82.3 4.6 broadcast_multiply_fusion
  86.9 7.6 gather_fusion
  94.5 4.1 copy.25
  98.6 3.3 copy.16
  101.9 5.6 all-to-all-start
  107.6 0.8 convert_reduce_fusion.1
  108.8 0.3 reduce-window.24
  109.7 0.3 compare_select_fusion
  110.0 452.2 %scatter_custom_fusion = s32[4096]{0:T(1024)S(1)} fusion(s32[65536]{0:T(1024)S(1)} %bitcast.103, s32[65536]{0:T(1024)S(1)} %ne.84, s32[]{:T(128)} %copy.53), kind=kCustom, calls=%fused_computation.94 | custom fusion | flops 65536 | bytes 16388 | tf_op jit(solution)/shard_map/scatter-add | solution.py:61
  562.2 0.3 reduce-window.31
  562.8 0.7 compare_select_fusion.2
  563.6 23.0 %gather_fusion.1 = s32[4096]{0:T(1024)S(1)} fusion(s32[65536]{0:T(1024)S(1)} %copy-done, s32[4096]{0:T(1024)S(1)} %broadcast_clamp_fusion), kind=kCustom, calls=%fused_computation.1 | custom fusion | bytes 49152 | tf_op jit(solution)/shard_map/gather | solution.py:62
  586.7 15.5 %scatter_custom_fusion.1 = s32[4096]{0:T(1024)S(1)} fusion(s32[4096]{0:T(1024)S(1)} %bitcast.108, s32[4096]{0:T(1024)S(1)} %iota.77, s32[]{:T(128)} %copy.53), kind=kCustom, calls=%fused_computation.92 | custom fusion | bytes 16388 | tf_op jit(solution)/shard_map/scatter | solution.py:64
  602.3 18.3 %gather_fusion.2 = f32[4096,256]{1,0:T(8,128)} fusion(f32[4096,256]{1,0:T(8,128)} %bitcast.4, s32[4096]{0:T(1024)S(1)} %fusion.28), kind=kCustom, calls=%fused_computation.2 | custom fusion | bytes 8404992 | tf_op jit(solution)/shard_map/gather | solution.py:66
  620.6 10.9 fusion.44
  631.8 84.2 %all-reduce.9.cloned.1.call-done = f32[256,256]{0,1:T(8,128)} async-done(((f32[256,256]{0,1:T(8,128)}), f32[256,256]{0,1:T(8,128)}) %all-reduce.9.cloned.1.call-update) | async-done | bytes 262160 | tf_op jit(solution)/shard_map/psum | solution.py:71
  716.0 1.1 copy.20
  717.1 1.0 fusion.10
  718.1 11.7 cholesky.130
  729.9 9.8 custom-call.13
  740.2 11.7 cholesky.147
  752.0 0.7 compare_reduce_fusion.2
  754.1 4.5 while.4
  754.6 0.6 fusion.73
  755.2 1.4 bitcast_dynamic-update-slice_fusion.4
  756.6 0.6 fusion.73
  757.2 1.4 bitcast_dynamic-update-slice_fusion.4
  758.7 19.7 %custom-call.14 = f32[2,128,128]{1,2,0:T(8,128)S(1)} custom-call(f32[2,128,128]{2,1,0:T(8,128)S(1)} %get-tuple-element.20), custom_call_target="InvertDiagBlocksLowerTriangular" | custom-call | tf_op jit(solution)/shard_map/jit(_solve_triangular)/triangular_solve | solution.py:20
  778.3 0.3 fusion.16
  778.9 0.3 fusion.23
  779.2 7.6 convolution_select_fusion.1
  786.9 72.0 %all-reduce.11.cloned.1.call-done = f32[4096,256]{1,0:T(8,128)} async-done(((f32[4096,256]{1,0:T(8,128)}), f32[4096,256]{1,0:T(8,128)}) %all-reduce.11.cloned.1.call-update) | async-done | bytes 4194320 | tf_op jit(solution)/shard_map/psum | solution.py:15
  859.0 10.9 fusion.45
  870.2 84.3 %all-reduce.13.cloned.1.call-done = f32[256,256]{1,0:T(8,128)} async-done(((f32[256,256]{1,0:T(8,128)}), f32[256,256]{1,0:T(8,128)}) %all-reduce.13.cloned.1.call-update) | async-done | bytes 262160 | tf_op jit(solution)/shard_map/psum | solution.py:73
  954.5 7.0 convolution_subtract_fusion.1
  961.5 2.0 copy-done.1
  963.5 7.4 fusion.46
  971.2 83.3 %all-reduce.15.cloned.1.call-done = f32[256,256]{0,1:T(8,128)} async-done(((f32[256,256]{0,1:T(8,128)}), f32[256,256]{0,1:T(8,128)}) %all-reduce.15.cloned.1.call-update) | async-done | bytes 262160 | tf_op jit(solution)/shard_map/psum | solution.py:71
  1054.5 1.1 copy.22
  1055.6 1.0 fusion.9
  1056.6 11.7 cholesky.164
  1068.3 9.8 custom-call.15
  1078.6 11.7 cholesky.181
  1090.4 0.7 compare_reduce_fusion
  1091.1 0.6 compare_reduce_fusion.1
  1093.1 4.5 while.5
  1093.6 0.6 fusion.74
  1094.2 1.4 bitcast_dynamic-update-slice_fusion.5
  1095.6 0.6 fusion.74
  1096.2 1.4 bitcast_dynamic-update-slice_fusion.5
  1097.7 19.7 %custom-call.16 = f32[2,128,128]{1,2,0:T(8,128)S(1)} custom-call(f32[2,128,128]{2,1,0:T(8,128)S(1)} %get-tuple-element.21), custom_call_target="InvertDiagBlocksLowerTriangular" | custom-call | tf_op jit(solution)/shard_map/jit(_solve_triangular)/triangular_solve | solution.py:20
  1117.3 0.3 fusion.14
  1117.9 0.3 fusion.19
  1118.3 7.6 convolution_select_fusion
  1126.1 71.9 %all-reduce.17.cloned.1.call-done = f32[4096,256]{1,0:T(8,128)} async-done(((f32[4096,256]{1,0:T(8,128)}), f32[4096,256]{1,0:T(8,128)}) %all-reduce.17.cloned.1.call-update) | async-done | bytes 4194320 | tf_op jit(solution)/shard_map/psum | solution.py:15
  1198.0 10.9 fusion.47
  1208.9 84.5 %all-reduce.19.cloned.1.call-done = f32[256,256]{1,0:T(8,128)} async-done(((f32[256,256]{1,0:T(8,128)}), f32[256,256]{1,0:T(8,128)}) %all-reduce.19.cloned.1.call-update) | async-done | bytes 262160 | tf_op jit(solution)/shard_map/psum | solution.py:73
  1293.5 9.0 convolution_subtract_fusion
  1302.5 0.8 pad_maximum_fusion
  (69 shorter events, 4.4 us)
Async XLA Ops:
  101.9 5.6 copy-start
  101.9 500.3 %all-to-all-start = ((f32[128,32,256]{2,1,0:T(8,128)}), f32[128,32,256]{2,1,0:T(8,128)}, u32[]{:S(2)}, u32[]{:S(2)}) async-start(f32[128,32,256]{2,1,0:T(8,128)} %bitcast.100), calls=%async_computation | async-start | bytes 8388608 | tf_op jit(solution)/shard_map/all_to_all | solution.py:52
  107.5 608.5 %all-reduce.9.cloned.1.call-start = ((), (), s32[]{:S(2)}) async-start(), calls=%async_computation.1 | async-start | bytes 524288 | tf_op jit(solution)/shard_map/psum | solution.py:71
  631.5 227.5 %all-reduce.11.cloned.1.call-start = ((), (), s32[]{:S(2)}) async-start(), calls=%async_computation.2 | async-start | bytes 8388608 | tf_op jit(solution)/shard_map/psum | solution.py:15
  786.9 167.6 %all-reduce.13.cloned.1.call-start = ((), (), s32[]{:S(2)}) async-start(), calls=%async_computation.3 | async-start | bytes 524288 | tf_op jit(solution)/shard_map/psum | solution.py:73
  869.9 184.6 %all-reduce.15.cloned.1.call-start = ((), (), s32[]{:S(2)}) async-start(), calls=%async_computation.4 | async-start | bytes 524288 | tf_op jit(solution)/shard_map/psum | solution.py:71
  961.5 2.0 copy-start.1
  970.9 227.1 %all-reduce.17.cloned.1.call-start = ((), (), s32[]{:S(2)}) async-start(), calls=%async_computation.5 | async-start | bytes 8388608 | tf_op jit(solution)/shard_map/psum | solution.py:15
  1125.9 167.6 %all-reduce.19.cloned.1.call-start = ((), (), s32[]{:S(2)}) async-start(), calls=%async_computation.6 | async-start | bytes 524288 | tf_op jit(solution)/shard_map/psum | solution.py:73
  1208.9 93.6 %copy-start.2 = (f32[256,256]{1,0:T(8,128)S(1)}, f32[256,256]{1,0:T(8,128)}, u32[]{:S(2)}) copy-start(f32[256,256]{1,0:T(8,128)} %all-reduce.13.cloned.1.call-done) | copy-start | bytes 786436
  1293.5 9.0 copy-start.3
Sparse Core Ops, SparseCore 0:
  631.6 84.3 all-reduce.8
  787.0 71.9 all-reduce.10
  870.1 84.3 all-reduce.12
  971.0 83.3 all-reduce.14
  1126.0 71.9 all-reduce.16
  1209.0 84.3 all-reduce.18
where the time goes:
time: 1320 us; the launch traced here: 1310 us
  other arithmetic  576 us (44%)
  waiting for transfers between devices  480 us (36%)
  local copies, waits for them, and re-layouts  85.1 us (6%)
  matrix products  75.2 us (6%)
  blocking collectives  68.7 us (5%)
  between operations  17.4 us (1%)
    scatter-add x1, other arithmetic, body(): chosen = jnp.nonzero(target // local_rows == my_row, size=local_rows)[0]  452 us
    psum x2, waiting for transfers between devices, body(): projection = lax.psum(jnp.dot(basis.T, block, precision=HIGH), 'row')  169 us
    psum x2, waiting for transfers between devices, body(): gram = lax.psum(gram_of(panel), 'row')  168 us
    psum x2, waiting for transfers between devices, from_root(): return lax.psum(kept, axis)  144 us
    psum x1, blocking collectives, body(): counts = lax.psum(jnp.sum(member, axis=0), ('row', 'col'))  68.7 us
    another operation x13, other arithmetic, orthonormal(): lower = jnp.linalg.cholesky(gram)  68.7 us
    another operation x5, other arithmetic, orthonormal(): jax.scipy.linalg.solve_triangular(lower, jnp.eye(gram.shape[0], dtype=gra...  39.4 us
  transfers between devices with their start and end apart: 7, of which 6 were waited for; matrix products, arithmetic and copies ran while one was open for 38% of the time, Pallas kernels for 0%

commit v1 on v0

v1 whole, which is shorter than its diff:
```python
import jax
import jax.numpy as jnp
from jax import lax
from jax.experimental import pallas as pl
from jax.experimental.pallas import tpu as pltpu
from jax.sharding import PartitionSpec as P

MESH = pl.DeviceIdType.MESH
NB = 256
PANELS = 2
K = PANELS * NB
DIST_MEAN = 256
HIGH = lax.Precision.HIGHEST
F32 = jnp.float32
BF16 = jnp.bfloat16
VMEM = pl.BlockSpec(memory_space=pltpu.VMEM)


def split2(x):
    hi = x.astype(BF16)
    return hi, (x - hi.astype(F32)).astype(BF16)


def dims(a, b):
    return (((a,), (b,)), ((), ()))


def mm(x, y, a=1, b=0):
    return lax.dot_general(x, y, dims(a, b), preferred_element_type=F32)


def mm3(xh, xl, yh, yl, a=1, b=0):
    return mm(xh, yh, a, b) + (mm(xh, yl, a, b) + mm(xl, yh, a, b))


def counts_kernel(district_ref, weight_ref, own, got, send_sem, recv_sem):
    row, col = lax.axis_index("row"), lax.axis_index("col")
    n_row, n_col = lax.axis_size("row"), lax.axis_size("col")
    n = n_row * n_col
    me = row * n_col + col
    steps = (n - 2, n - 1, 1, 2)

    def peer(step):
        other = lax.rem(me + step, n)
        return other // n_col, lax.rem(other, n_col)

    barrier = pltpu.get_barrier_semaphore()
    for step in steps:
        pl.semaphore_signal(barrier, inc=1, device_id=peer(step), device_id_type=MESH)
    nodes = district_ref.shape[0]
    lanes = lax.broadcasted_iota(jnp.int32, (nodes, 256), 1)
    member = district_ref[...] == lanes
    hist = jnp.sum(jnp.where(member, 1.0, 0.0), axis=0, keepdims=True)
    own[...] = jnp.broadcast_to(hist, own.shape)
    pl.semaphore_wait(barrier, 4)
    copies = []
    for k, step in enumerate(steps):
        copy = pltpu.make_async_remote_copy(
            own, got.at[k], send_sem.at[k], recv_sem.at[k], device_id=peer(step), device_id_type=MESH
        )
        copy.start()
        copies.append(copy)
    for copy in copies:
        copy.wait()
    total = own[...]
    valid = (me + 2 < n, me + 1 < n, me >= 1, me >= 2)
    for k in range(4):
        total = total + got[k] * jnp.where(valid[k], 1.0, 0.0)
    scale = jnp.sqrt(DIST_MEAN / jnp.maximum(total, 1.0))[0:1, :]
    weight_ref[...] = jnp.sum(jnp.where(member, scale, 0.0), axis=1, keepdims=True)


def weights_of(district):
    nodes = district.shape[0]
    return pl.pallas_call(
        counts_kernel,
        out_shape=jax.ShapeDtypeStruct((nodes, 1), F32),
        in_specs=[VMEM],
        out_specs=VMEM,
        scratch_shapes=[
            pltpu.VMEM((8, 256), F32),
            pltpu.VMEM((4, 8, 256), F32),
            pltpu.SemaphoreType.DMA((4,)),
            pltpu.SemaphoreType.DMA((4,)),
        ],
        compiler_params=pltpu.CompilerParams(collective_id=0, has_side_effects=True),
        name="counts",
    )(district.reshape(nodes, 1))


def prep_kernel(local_rows, n_row, panel_ref, x_ref, weight_ref, target_ref, rows_ref, gram_ref, left_hi, left_lo, perm):
    nodes = x_ref.shape[0]
    per = nodes // n_row

    @pl.when(pl.program_id(0) == 0)
    def _():
        left = panel_ref[...] * weight_ref[...]
        hi, lo = split2(left)
        left_hi[...] = hi.T
        left_lo[...] = lo.T
        owner = target_ref[...] // local_rows
        groups = lax.broadcasted_iota(jnp.int32, (n_row, nodes), 0)
        mask = jnp.where(owner == groups, 1.0, 0.0)
        before = jnp.where(
            lax.broadcasted_iota(jnp.int32, (nodes, nodes), 0) < lax.broadcasted_iota(jnp.int32, (nodes, nodes), 1), 1.0, 0.0
        ).astype(BF16)
        rank = mm(mask.astype(BF16), before)
        base = groups.astype(F32) * per
        place = jnp.sum(mask * (rank + base), axis=0, keepdims=True).astype(jnp.int32)
        perm[...] = jnp.where(place == lax.broadcasted_iota(jnp.int32, (nodes, nodes), 0), 1.0, 0.0).astype(BF16)

    x = x_ref[...] * weight_ref[...]
    hi = x.astype(BF16)
    rest = x - hi.astype(F32)
    mid = rest.astype(BF16)
    low = (rest - mid.astype(F32)).astype(BF16)
    p = perm[...]
    rows_ref[...] = (mm(p, hi) + mm(p, mid)) + mm(p, low)
    gram_ref[...] = mm3(left_hi[...], left_lo[...], hi, mid)


def prep(snapshots, weight, mine, n_row, local_rows):
    nodes, snaps = snapshots.shape
    out = jax.ShapeDtypeStruct((nodes, snaps), F32), jax.ShapeDtypeStruct((K, snaps), F32)
    return pl.pallas_call(
        lambda *refs: prep_kernel(local_rows, n_row, *refs),
        grid=(snaps // NB,),
        out_shape=out,
        in_specs=[
            pl.BlockSpec((nodes, K), lambda i: (0, 0)),
            pl.BlockSpec((nodes, NB), lambda i: (0, i)),
            pl.BlockSpec((nodes, 1), lambda i: (0, 0)),
            pl.BlockSpec((1, nodes), lambda i: (0, 0)),
        ],
        out_specs=(pl.BlockSpec((nodes, NB), lambda i: (0, i)), pl.BlockSpec((K, NB), lambda i: (0, i))),
        scratch_shapes=[pltpu.VMEM((K, nodes), BF16), pltpu.VMEM((K, nodes), BF16), pltpu.VMEM((nodes, nodes), BF16)],
        compiler_params=pltpu.CompilerParams(vmem_limit_bytes=32 << 20),
        name="prep",
    )(snapshots, snapshots, weight, mine.reshape(1, nodes))


def sum_kernel(a_ref, out_ref, acc, got0, got1, got2, got3, send_sem, recv_sem):
    row, col = lax.axis_index("row"), lax.axis_index("col")
    y, x, z, core = row // 4, lax.rem(row, 4), col // 2, lax.rem(col, 2)
    half = a_ref.shape[0] // 2
    q1, q2 = half // 4, half // 16
    width = a_ref.shape[1] // 4
    first = (1 - core) * x + core * y
    second = (1 - core) * y + core * x

    def pair(p, q):
        return ((1 - core) * q + core * p) * 4 + (1 - core) * p + core * q

    def peer1(d):
        return pair(lax.rem(first + d, 4), second), col

    def peer2(d):
        return pair(first, lax.rem(second + d, 4)), col

    def peer3(d):
        return row, lax.rem(z + d, 4) * 2 + core

    sibling = (row, z * 2 + 1 - core)
    barrier = pltpu.get_barrier_semaphore()
    everyone = [sibling] + [peer(d) for peer in (peer1, peer2, peer3) for d in (1, 2, 3)]
    for one in everyone:
        pl.semaphore_signal(barrier, inc=1, device_id=one, device_id_type=MESH)
    pl.semaphore_wait(barrier, len(everyone))

    def send(src, dst, slot, to):
        copy = pltpu.make_async_remote_copy(src, dst, send_sem.at[slot], recv_sem.at[slot], device_id=to, device_id_type=MESH)
        copy.start()
        return copy

    def rows(start, size):
        return pl.ds(pl.multiple_of(start, size), size)

    mine = core * half
    copy = send(a_ref.at[rows((1 - core) * half, half), :], got0, 0, sibling)
    copy.wait()
    acc[...] = a_ref[rows(mine, half), :] + got0[...]

    copies = [
        send(acc.at[rows(lax.rem(first + d, 4) * q1, q1), :], got1.at[d - 1], d, peer1(d)) for d in (1, 2, 3)
    ]
    for copy in copies:
        copy.wait()
    at1 = first * q1
    acc[rows(at1, q1), :] = (acc[rows(at1, q1), :] + got1[0]) + (got1[1] + got1[2])

    copies = [
        send(acc.at[rows(at1 + lax.rem(second + d, 4) * q2, q2), :], got2.at[d - 1], 3 + d, peer2(d)) for d in (1, 2, 3)
    ]
    for copy in copies:
        copy.wait()
    at2 = at1 + second * q2
    acc[rows(at2, q2), :] = (acc[rows(at2, q2), :] + got2[0]) + (got2[1] + got2[2])

    def columns(index):
        return pl.ds(pl.multiple_of(index * width, width), width)

    copies = [
        send(acc.at[rows(at2, q2), columns(lax.rem(z + d, 4))], got3.at[d - 1], 6 + d, peer3(d)) for d in (1, 2, 3)
    ]
    for copy in copies:
        copy.wait()
    out_ref[rows(mine + at2, q2), columns(z)] = (acc[rows(at2, q2), columns(z)] + got3[0]) + (got3[1] + got3[2])

    piece = out_ref.at[rows(mine + at2, q2), columns(z)]
    copies = [send(piece, piece, 9 + d, peer3(d)) for d in (1, 2, 3)]
    for copy in copies:
        copy.wait()
    piece = out_ref.at[rows(mine + at2, q2), :]
    copies = [send(piece, piece, 12 + d, peer2(d)) for d in (1, 2, 3)]
    for copy in copies:
        copy.wait()
    piece = out_ref.at[rows(mine + at1, q1), :]
    copies = [send(piece, piece, 15 + d, peer1(d)) for d in (1, 2, 3)]
    for copy in copies:
        copy.wait()
    piece = out_ref.at[rows(mine, half), :]
    copy = send(piece, piece, 19, sibling)
    copy.wait()


def sum_all(a):
    k, snaps = a.shape
    half = k // 2
    return pl.pallas_call(
        sum_kernel,
        out_shape=jax.ShapeDtypeStruct(a.shape, F32),
        in_specs=[VMEM],
        out_specs=VMEM,
        scratch_shapes=[
            pltpu.VMEM((half, snaps), F32),
            pltpu.VMEM((half, snaps), F32),
            pltpu.VMEM((3, half // 4, snaps), F32),
            pltpu.VMEM((3, half // 16, snaps), F32),
            pltpu.VMEM((3, half // 16, snaps // 4), F32),
            pltpu.SemaphoreType.DMA((20,)),
            pltpu.SemaphoreType.DMA((20,)),
        ],
        compiler_params=pltpu.CompilerParams(collective_id=1, has_side_effects=True, vmem_limit_bytes=32 << 20),
        name="sum_gram",
    )(a)


def factor_kernel(gram_ref, inverse_ref, work):
    b = 128
    work[:, :K] = gram_ref[...]
    r = lax.broadcasted_iota(jnp.int32, (K, K), 0)
    c = lax.broadcasted_iota(jnp.int32, (K, K), 1)
    work[:, K:] = jnp.where(r == c, 1.0, 0.0)
    sub = lax.broadcasted_iota(jnp.int32, (8, b), 0)
    lane = lax.broadcasted_iota(jnp.int32, (8, b), 1)
    groups = b // 8

    def block(k, carry):
        start = pl.multiple_of(k * b, b)
        s = [work[pl.ds(pl.multiple_of(start + 8 * g, 8), 8), pl.ds(start, b)] for g in range(groups)]
        e = [jnp.where(lane == sub + 8 * g, 1.0, 0.0) for g in range(groups)]
        t = [jnp.zeros((8, b), F32)] * groups
        for j in range(b):
            g0, r0 = j // 8, j % 8
            line = jnp.broadcast_to(s[g0][r0 : r0 + 1, :], (8, b))
            eline = jnp.broadcast_to(e[g0][r0 : r0 + 1, :], (8, b))
            pivot = jnp.broadcast_to(line[:, j : j + 1], (8, b))
            inv = 1.0 / pivot
            t[g0] = jnp.where(sub == r0, eline * lax.rsqrt(pivot), t[g0])
            line = line * inv
            eline = eline * inv
            for g in range(g0, groups):
                if g == g0 and r0 == 7:
                    continue
                m = jnp.broadcast_to(s[g][:, j : j + 1], (8, b))
                if g == g0:
                    m = jnp.where(sub > r0, m, 0.0)
                s[g] = s[g] - m * line
                e[g] = e[g] - m * eline
        top = jnp.concatenate(t, axis=0)
        upper = jnp.dot(top, work[pl.ds(start, b), :], precision=HIGH, preferred_element_type=F32)
        work[pl.ds(start, b), :] = upper
        inverse_ref[pl.ds(start, b), :] = upper[:, K:]
        left = work[pl.ds(start, b), :K]
        after = lax.broadcasted_iota(jnp.int32, (b, K), 1) >= start + b
        left = jnp.where(after, left, 0.0)
        work[...] = work[...] - lax.dot_general(left, upper, dims(0, 0), precision=HIGH, preferred_element_type=F32)
        return carry

    lax.fori_loop(0, K // b, block, 0)


def factor(gram):
    return pl.pallas_call(
        factor_kernel,
        grid=(1,),
        out_shape=jax.ShapeDtypeStruct((K, K), F32),
        in_specs=[pl.BlockSpec((K, K), lambda i: (0, 0))],
        out_specs=pl.BlockSpec((K, K), lambda i: (0, 0)),
        scratch_shapes=[pltpu.VMEM((K, 2 * K), F32)],
        compiler_params=pltpu.CompilerParams(vmem_limit_bytes=32 << 20),
        name="factor",
    )(gram)


def update_kernel(inverse_ref, left_ref, rows_ref, gram_ref, rest_ref, coef_ref, inv_hi, inv_lo, q_hi, q_lo):
    @pl.when(pl.program_id(0) == 0)
    def _():
        hi, lo = split2(inverse_ref[...])
        inv_hi[...], inv_lo[...] = hi, lo
        left_hi, left_lo = split2(left_ref[...])
        q = mm3(left_hi, left_lo, hi, lo, 1, 1)
        q_hi[...], q_lo[...] = split2(q)

    g_hi, g_lo = split2(gram_ref[...])
    coef = mm3(inv_hi[...], inv_lo[...], g_hi, g_lo)
    coef_ref[...] = coef
    c_hi, c_lo = split2(coef)
    rest = rows_ref[...] - mm3(q_hi[...], q_lo[...], c_hi, c_lo)
    rest_ref[...] = rest.reshape(rest_ref.shape)


def update(inverse, rows, gram, n_row):
    nodes, snaps = rows.shape
    n_blocks = snaps // NB
    per = nodes // n_row
    return pl.pallas_call(
        update_kernel,
        grid=(n_blocks,),
        out_shape=(
            jax.ShapeDtypeStruct((n_row, n_blocks, per, NB), F32),
            jax.ShapeDtypeStruct((K, snaps), F32),
        ),
        in_specs=[
            pl.BlockSpec((K, K), lambda i: (0, 0)),
            pl.BlockSpec((nodes, K), lambda i: (0, 0)),
            pl.BlockSpec((nodes, NB), lambda i: (0, i)),
            pl.BlockSpec((K, NB), lambda i: (0, i)),
        ],
        out_specs=(
            pl.BlockSpec((n_row, 1, per, NB), lambda i: (0, i, 0, 0)),
            pl.BlockSpec((K, NB), lambda i: (0, i)),
        ),
        scratch_shapes=[pltpu.VMEM((K, K), BF16)] * 2 + [pltpu.VMEM((nodes, K), BF16)] * 2,
        compiler_params=pltpu.CompilerParams(vmem_limit_bytes=32 << 20),
        name="update",
    )(inverse, rows, rows, gram)


def route_kernel(local_rows, per, target_ref, place_ref):
    row = lax.axis_index("row")
    target = target_ref[...]
    n, nodes = target.shape
    mask = jnp.where(target // local_rows == row, 1.0, 0.0)
    before = jnp.where(
        lax.broadcasted_iota(jnp.int32, (nodes, nodes), 0) < lax.broadcasted_iota(jnp.int32, (nodes, nodes), 1), 1.0, 0.0
    ).astype(BF16)
    rank = mm(mask.astype(BF16), before)
    rank = jnp.where(mask > 0.0, rank, -1.0)
    value = lax.rem(target, local_rows).astype(F32)
    lanes = lax.broadcasted_iota(jnp.int32, (n, per), 1)
    place = jnp.zeros((n, per), F32)
    for k in range(per):
        one = jnp.sum(jnp.where(rank == k, value, 0.0), axis=1, keepdims=True)
        place = jnp.where(lanes == k, one, place)
    place_ref[...] = place.astype(jnp.int32)


def route(target, n, local_rows, per):
    return pl.pallas_call(
        lambda *refs: route_kernel(local_rows, per, *refs),
        out_shape=jax.ShapeDtypeStruct((n, per), jnp.int32),
        in_specs=[VMEM],
        out_specs=VMEM,
        name="route",
    )(target.reshape(n, -1))


def place_kernel(place_ref, rows_ref, out_ref):
    n, per = place_ref.shape

    def body(s, carry):
        for k in range(per):
            out_ref[pl.ds(place_ref[s, k], 1), :] = rows_ref[pl.ds(s * per + k, 1), :]
        return carry

    lax.fori_loop(0, n, body, 0)


def place_rows(place, rows):
    return pl.pallas_call(
        place_kernel,
        out_shape=jax.ShapeDtypeStruct(rows.shape, F32),
        in_specs=[pl.BlockSpec(memory_space=pltpu.SMEM), VMEM],
        out_specs=VMEM,
        compiler_params=pltpu.CompilerParams(vmem_limit_bytes=32 << 20),
        name="place",
    )(place, rows)


def body(snapshots, district, target):
    n_row, n_col = lax.axis_size("row"), lax.axis_size("col")
    n = n_row * n_col
    nodes_dev, snaps = snapshots.shape
    local_rows = target.shape[0] // n_row
    per = nodes_dev // n_row
    me = lax.axis_index(("row", "col"))
    mine = lax.dynamic_slice_in_dim(target, me * nodes_dev, nodes_dev)
    weight = weights_of(district)
    rows, gram = prep(snapshots, weight, mine, n_row, local_rows)
    place = route(target, n, local_rows, per)
    gram = sum_all(gram)
    inverse = factor(gram)
    rest, coef = update(inverse, rows, gram, n_row)
    moved = lax.all_to_all(rest.reshape(n, per, NB), ("row", "col"), split_axis=0, concat_axis=0, tiled=True)
    remainder = place_rows(place, moved.reshape(n * per, NB))
    coefficients = lax.dynamic_slice_in_dim(coef, lax.axis_index("col") * NB, NB, axis=1)
    return coefficients, remainder


def solution(mesh):
    in_specs = (P(("row", "col"), None), P(("row", "col")), P())
    out_specs = (P(None, "col"), P("row", "col"))
    return jax.shard_map(body, mesh=mesh, in_specs=in_specs, out_specs=out_specs, check_vma=False)
```

time: 1320 us -> 276 us (0.21)
  other arithmetic: 576 us -> 0 us
  waiting for transfers between devices: 480 us -> 47.3 us
  Pallas kernels: 0 us -> 206 us
  matrix products: 75.2 us -> 0 us
  local copies, waits for them, and re-layouts: 85.1 us -> 12.9 us
  blocking collectives: 68.7 us -> 0 us
  between operations: 17.4 us -> 0.71 us
    psum x6 -> x0, waiting for transfers between devices: 480 us -> none  [the longest x2 169 us: body(): projection = lax.psum(jnp.dot(basis.T, block, precision=HIGH), 'row')]
    scatter-add x1 -> x0, other arithmetic: 452 us -> none  [body(): chosen = jnp.nonzero(target // local_rows == my_row, size=local_rows)[0]]
    pallas_call x0 -> x7, Pallas kernels: none -> 206 us  [the longest x1 77.7 us: factor(): pl.pallas_call(factor_kernel, grid=(1,), out_shape=jax.ShapeDtypeStruct((...]
    another operation x27 -> x0, other arithmetic: 109 us -> none  [the longest x13 68.7 us: orthonormal(): lower = jnp.linalg.cholesky(gram)]
    dot_general x9 -> x0, matrix products: 72.4 us -> none  [the longest x2 21.8 us: body(): projection = lax.psum(jnp.dot(basis.T, block, precision=HIGH), 'row')]
    psum x1 -> x0, blocking collectives: 68.7 us -> none  [body(): counts = lax.psum(jnp.sum(member, axis=0), ('row', 'col'))]
    gather x3 -> x0, local copies, waits for them, and re-layouts: 48.9 us -> none  [the longest x1 23 us: body(): placing = target[chosen] % local_rows]
    all_to_all x1, waiting for transfers between devices: 0.01 us -> 47.3 us  [body(): lax.all_to_all(rest.reshape(n, per, NB), ('row', 'col'), split_axis=0, co...]
  transfers between devices with their start and end apart: 7 -> 1, of which waited for: 6 -> 1; matrix products, arithmetic and copies ran while one was open for 38% -> 1% of each run, Pallas kernels for 0% -> 1%
where the time goes in v1:
time: 276 us
  Pallas kernels  206 us (75%)
  waiting for transfers between devices  47.3 us (17%)
  local copies, waits for them, and re-layouts  12.9 us (5%)
  starting transfers between devices  8.99 us (3%)
    pallas_call x1, Pallas kernels, factor(): pl.pallas_call(factor_kernel, grid=(1,), out_shape=jax.ShapeDtypeStruct((...  77.7 us
    pallas_call x1, Pallas kernels, sum_all(): pl.pallas_call(sum_kernel, out_shape=jax.ShapeDtypeStruct(a.shape, F32),...  66.5 us
    all_to_all x1, waiting for transfers between devices, body(): lax.all_to_all(rest.reshape(n, per, NB), ('row', 'col'), split_axis=0, co...  47.3 us
    pallas_call x1, Pallas kernels, place_rows(): pl.pallas_call(place_kernel, out_shape=jax.ShapeDtypeStruct(rows.shape, F...  18.9 us
    pallas_call x1, Pallas kernels, update(): pl.pallas_call(update_kernel, grid=(n_blocks,), out_shape=(jax.ShapeDtype...  16.9 us
    pallas_call x1, Pallas kernels, weights_of(): pl.pallas_call(counts_kernel, out_shape=jax.ShapeDtypeStruct((nodes, 1),...  13.1 us
    pallas_call x1, Pallas kernels, prep(): pl.pallas_call(lambda *refs: prep_kernel(local_rows, n_row, *refs), grid=...  10.1 us
    all_to_all x1, starting transfers between devices, body(): lax.all_to_all(rest.reshape(n, per, NB), ('row', 'col'), split_axis=0, co...  8.99 us
  transfers between devices with their start and end apart: 1, of which 1 were waited for; matrix products, arithmetic and copies ran while one was open for 1% of the time, Pallas kernels for 1%

profile of v1, /device:TPU:1, one launch (start us, length us, event | category | flops | bytes accessed | tf_op | source)
XLA Modules:
  0.0 275.9 jit_solution(2422536676985394814)
XLA Ops:
  0.6 1.5 copy.5.district_ref
  2.2 13.1 %counts.1.refs_2_ = f32[512,1]{1,0:T(8,128)} custom-call(s32[512,1]{1,0:T(8,128)} %copy.5.district_ref), custom_call_target="tpu_custom_call" | custom-call | tf_op jit(solution)/shard_map/counts/pallas_call | solution.py:75
  15.3 0.8 dynamic_slice.6
  16.1 0.0 copy-start
  16.1 2.2 copy-done
  18.3 0.0 copy-start.2
  18.3 0.9 copy-done.2
  19.2 10.1 %prep.1 = (f32[512,2048]{1,0:T(8,128)S(1)}, f32[512,2048]{1,0:T(8,128)S(1)}) custom-call(f32[512,2048]{1,0:T(8,128)S(1)} %copy-done, f32[512,2048]{1,0:T(8,128)S(1)} %copy-done, f32[512,1]{1,0:T(8,128)S(1)} %copy-done.2, s32[1,512]{1,0:T(1,128)S(1)} %bitcast.5), custom_call_target="tpu_custom_call" | custom-call | tf_op jit(solution)/shard_map/prep/pallas_call | solution.py:125
  29.3 66.5 %sum_gram.1.gram_ref = f32[512,2048]{1,0:T(8,128)S(1)} custom-call(f32[512,2048]{1,0:T(8,128)S(1)} %get-tuple-element.6.a_ref), custom_call_target="tpu_custom_call" | custom-call | tf_op jit(solution)/shard_map/sum_gram/pallas_call | solution.py:229
  95.8 77.7 %factor.1.inverse_ref = f32[512,512]{1,0:T(8,128)S(1)} custom-call(f32[512,2048]{1,0:T(8,128)S(1)} %sum_gram.1.gram_ref), custom_call_target="tpu_custom_call" | custom-call | tf_op jit(solution)/shard_map/factor/pallas_call | solution.py:294
  173.6 16.9 %update.1 = (f32[16,8,32,256]{3,2,1,0:T(8,128)S(1)}, f32[512,2048]{1,0:T(8,128)S(1)}) custom-call(f32[512,512]{1,0:T(8,128)S(1)} %factor.1.inverse_ref, f32[512,2048]{1,0:T(8,128)S(1)} %get-tuple-element.7.left_ref.rows_ref, f32[512,2048]{1,0:T(8,128)S(1)} %get-tuple-element.7.left_ref.rows_ref, f32[512,2048]{1,0:T(8,128)S(1)} %sum_gram.1.gram_ref), custom_call_target="tpu_custom_call" | custom-call | tf_op jit(solution)/shard_map/update/pallas_call | solution.py:327
  190.5 0.0 copy-start.1
  190.5 2.0 copy-done.1
  192.5 0.0 copy-start.4
  192.5 2.0 copy-done.4
  194.5 0.0 copy-start.5
  194.5 9.0 %all-to-all-start = ((f32[128,32,256]{2,1,0:T(8,128)}), f32[128,32,256]{2,1,0:T(8,128)}, u32[]{:S(2)}, u32[]{:S(2)}) async-start(f32[128,32,256]{2,1,0:T(8,128)} %bitcast.4), calls=%async_computation | async-start | bytes 8388608 | tf_op jit(solution)/shard_map/all_to_all | solution.py:415
  203.5 0.0 copy-done.5
  203.5 0.7 reshape.21.refs_0_
  204.3 2.7 route.1.place_ref
  207.0 1.9 constant_dynamic-slice_fusion
  208.9 47.3 %all-to-all-done = f32[128,32,256]{2,1,0:T(8,128)} async-done(((f32[128,32,256]{2,1,0:T(8,128)}), f32[128,32,256]{2,1,0:T(8,128)}, u32[]{:S(2)}, u32[]{:S(2)}) %all-to-all-start) | async-done | bytes 4194336 | tf_op jit(solution)/shard_map/all_to_all | solution.py:415
  256.1 0.0 copy-start.3
  256.1 0.8 copy-done.3
  257.0 18.9 %place.1 = f32[4096,256]{1,0:T(8,128)} custom-call(s32[128,32]{1,0:T(8,128)S(1)} %copy-done.3, f32[4096,256]{1,0:T(8,128)} %bitcast.3.rows_ref), custom_call_target="tpu_custom_call" | custom-call | tf_op jit(solution)/shard_map/place/pallas_call | solution.py:391
Async XLA Ops:
  16.1 2.2 copy-start
  18.3 0.9 copy-start.2
  190.5 2.0 copy-start.1
  192.5 2.0 copy-start.4
  194.5 9.0 %copy-start.5 = (s32[65536]{0:T(1024)S(1)}, s32[65536]{0:T(1024)}, u32[]{:S(2)}) copy-start(s32[65536]{0:T(1024)} %param.5) | copy-start | bytes 786436
  194.5 61.6 %all-to-all-start = ((f32[128,32,256]{2,1,0:T(8,128)}), f32[128,32,256]{2,1,0:T(8,128)}, u32[]{:S(2)}, u32[]{:S(2)}) async-start(f32[128,32,256]{2,1,0:T(8,128)} %bitcast.4), calls=%async_computation | async-start | bytes 8388608 | tf_op jit(solution)/shard_map/all_to_all | solution.py:415
  256.1 0.8 copy-start.3

commit v2 on v1

--- a/solution.py
+++ b/solution.py
@@ -245,50 +245,67 @@
     )(a)
 
 
-def factor_kernel(gram_ref, inverse_ref, work):
-    b = 128
-    work[:, :K] = gram_ref[...]
-    r = lax.broadcasted_iota(jnp.int32, (K, K), 0)
-    c = lax.broadcasted_iota(jnp.int32, (K, K), 1)
-    work[:, K:] = jnp.where(r == c, 1.0, 0.0)
-    sub = lax.broadcasted_iota(jnp.int32, (8, b), 0)
-    lane = lax.broadcasted_iota(jnp.int32, (8, b), 1)
-    groups = b // 8
-
-    def block(k, carry):
-        start = pl.multiple_of(k * b, b)
-        s = [work[pl.ds(pl.multiple_of(start + 8 * g, 8), 8), pl.ds(start, b)] for g in range(groups)]
-        e = [jnp.where(lane == sub + 8 * g, 1.0, 0.0) for g in range(groups)]
-        t = [jnp.zeros((8, b), F32)] * groups
-        for j in range(b):
-            g0, r0 = j // 8, j % 8
-            line = jnp.broadcast_to(s[g0][r0 : r0 + 1, :], (8, b))
-            eline = jnp.broadcast_to(e[g0][r0 : r0 + 1, :], (8, b))
-            pivot = jnp.broadcast_to(line[:, j : j + 1], (8, b))
-            inv = 1.0 / pivot
-            t[g0] = jnp.where(sub == r0, eline * lax.rsqrt(pivot), t[g0])
-            line = line * inv
-            eline = eline * inv
-            for g in range(g0, groups):
-                if g == g0 and r0 == 7:
-                    continue
-                m = jnp.broadcast_to(s[g][:, j : j + 1], (8, b))
-                if g == g0:
-                    m = jnp.where(sub > r0, m, 0.0)
-                s[g] = s[g] - m * line
-                e[g] = e[g] - m * eline
-        top = jnp.concatenate(t, axis=0)
-        upper = jnp.dot(top, work[pl.ds(start, b), :], precision=HIGH, preferred_element_type=F32)
-        work[pl.ds(start, b), :] = upper
-        inverse_ref[pl.ds(start, b), :] = upper[:, K:]
-        left = work[pl.ds(start, b), :K]
-        after = lax.broadcasted_iota(jnp.int32, (b, K), 1) >= start + b
-        left = jnp.where(after, left, 0.0)
-        work[...] = work[...] - lax.dot_general(left, upper, dims(0, 0), precision=HIGH, preferred_element_type=F32)
+def hdot(x, y, a=1, b=0):
+    return lax.dot_general(x, y, dims(a, b), precision=HIGH, preferred_element_type=F32)
+
+
+def eliminate(work, top, start):
+    b=128; groups=b//8
+    sub=lax.broadcasted_iota(jnp.int32,(8,b),0); lane=lax.broadcasted_iota(jnp.int32,(8,b),1)
+    x=[work[pl.ds(pl.multiple_of(start+8*g,8),8), pl.ds(start,b)] for g in range(groups)]
+    for g0 in range(groups):
+        first=8*g0
+        column=[[jnp.broadcast_to(x[g][:,first+c:first+c+1],(8,b)) for c in range(8)] for g in range(g0,groups)]
+        inside=(lane>=first)&(lane<first+8)
+        own=jnp.where(inside,jnp.where(lane-first==sub,1.0,0.0),x[g0])
+        y=[jnp.broadcast_to(own[c:c+1,:],(8,b)) for c in range(8)]
+        d=[[jnp.broadcast_to(column[0][k][c:c+1,:],(8,b)) for k in range(c+1)] for c in range(8)]
+        inv=[]; low=[[None]*8 for _ in range(8)]
+        for k in range(8):
+            inv.append(1.0/d[k][k])
+            for c in range(k+1,8):
+                low[c][k]=d[c][k]*inv[k]
+            for c in range(k+1,8):
+                for m in range(k+1,c+1):
+                    d[c][m]=d[c][m]-low[c][k]*d[m][k]
+                y[c]=y[c]-low[c][k]*y[k]
+        t=jnp.zeros((8,b),F32)
+        for c in range(8):
+            t=jnp.where(sub==c,y[c]*lax.rsqrt(d[c][c]),t)
+        top[pl.ds(first,8),:]=jnp.where(lane<first+8,t,0.0)
+        v=[None]*8
+        for c in reversed(range(8)):
+            a=y[c]*inv[c]
+            for k in reversed(range(c+1,8)):
+                a=a-low[k][c]*v[k]
+            v[c]=a
+        for g in range(g0+1,groups):
+            m=column[g-g0]
+            u=[m[c]*v[c] for c in range(8)]
+            s=((u[0]+u[1])+(u[2]+u[3]))+((u[4]+u[5])+(u[6]+u[7]))
+            x[g]=jnp.where(inside,0.0,x[g])-s
+def factor_kernel(gram_ref, inverse_ref, work, top, upper):
+    b=128
+    work[...]=gram_ref[...]
+    n=K//b
+    def block(k,carry):
+        start=pl.multiple_of(k*b,b)
+        eliminate(work,top,start)
+        cols=lax.broadcasted_iota(jnp.int32,(b,K),1)
+        here=(cols>=start)&(cols<start+b)
+        rows=lax.broadcasted_iota(jnp.int32,(b,K),0)
+        line=jnp.where(here,jnp.where(cols-start==rows,1.0,0.0),work[pl.ds(start,b),:])
+        up=hdot(top[...],line)
+        upper[...]=up
+        inverse_ref[pl.ds(start,b),:]=jnp.where(cols<start+b,up,0.0)
+        def below(i,c):
+            at=pl.multiple_of(i*b,b)
+            left=upper[:,pl.ds(at,b)]
+            work[pl.ds(at,b),:]=jnp.where(here,0.0,work[pl.ds(at,b),:])-hdot(left,upper[...],0,0)
+            return c
+        lax.fori_loop(k+1,n,below,0)
         return carry
-
-    lax.fori_loop(0, K // b, block, 0)
-
+    lax.fori_loop(0,n,block,0)
 
 def factor(gram):
     return pl.pallas_call(
@@ -297,7 +314,7 @@
         out_shape=jax.ShapeDtypeStruct((K, K), F32),
         in_specs=[pl.BlockSpec((K, K), lambda i: (0, 0))],
         out_specs=pl.BlockSpec((K, K), lambda i: (0, 0)),
-        scratch_shapes=[pltpu.VMEM((K, 2 * K), F32)],
+        scratch_shapes=[pltpu.VMEM((K, K), F32), pltpu.VMEM((128, 128), F32), pltpu.VMEM((128, K), F32)],
         compiler_params=pltpu.CompilerParams(vmem_limit_bytes=32 << 20),
         name="factor",
     )(gram)
@@ -376,15 +393,27 @@
     )(target.reshape(n, -1))
 
 
-def place_kernel(place_ref, rows_ref, out_ref):
+def place_kernel(place_ref, rows_ref, out_ref, inverse):
     n, per = place_ref.shape
 
-    def body(s, carry):
+    def invert(s, carry):
         for k in range(per):
-            out_ref[pl.ds(place_ref[s, k], 1), :] = rows_ref[pl.ds(s * per + k, 1), :]
+            inverse[place_ref[s, k]] = s * per + k
         return carry
 
-    lax.fori_loop(0, n, body, 0)
+    lax.fori_loop(0, n, invert, 0)
+    sub = lax.broadcasted_iota(jnp.int32, (8, NB), 0)
+
+    def body(i, carry):
+        for u in range(4):
+            at = pl.multiple_of((i * 4 + u) * 8, 8)
+            rows = jnp.broadcast_to(rows_ref[pl.ds(inverse[at], 1), :], (8, NB))
+            for k in range(1, 8):
+                rows = jnp.where(sub == k, jnp.broadcast_to(rows_ref[pl.ds(inverse[at + k], 1), :], (8, NB)), rows)
+            out_ref[pl.ds(at, 8), :] = rows
+        return carry
+
+    lax.fori_loop(0, rows_ref.shape[0] // 32, body, 0)
 
 
 def place_rows(place, rows):
@@ -393,6 +422,7 @@
         out_shape=jax.ShapeDtypeStruct(rows.shape, F32),
         in_specs=[pl.BlockSpec(memory_space=pltpu.SMEM), VMEM],
         out_specs=VMEM,
+        scratch_shapes=[pltpu.SMEM((rows.shape[0],), jnp.int32)],
         compiler_params=pltpu.CompilerParams(vmem_limit_bytes=32 << 20),
         name="place",
     )(place, rows)

time: 276 us -> 222 us (0.80)
  Pallas kernels: 206 us -> 152 us
    pallas_call x1, Pallas kernels: 77.7 us -> 23.7 us  [factor(): pl.pallas_call(factor_kernel, grid=(1,), out_shape=jax.ShapeDtypeStruct((...]
where the time goes in v2:
time: 222 us
  Pallas kernels  152 us (68%)
  waiting for transfers between devices  47.3 us (21%)
  local copies, waits for them, and re-layouts  12.9 us (6%)
  starting transfers between devices  8.99 us (4%)
    pallas_call x1, Pallas kernels, sum_all(): pl.pallas_call(sum_kernel, out_shape=jax.ShapeDtypeStruct(a.shape, F32),...  66.5 us
    all_to_all x1, waiting for transfers between devices, body(): lax.all_to_all(rest.reshape(n, per, NB), ('row', 'col'), split_axis=0, co...  47.3 us
    pallas_call x1, Pallas kernels, factor(): pl.pallas_call(factor_kernel, grid=(1,), out_shape=jax.ShapeDtypeStruct((...  23.7 us
    pallas_call x1, Pallas kernels, place_rows(): pl.pallas_call(place_kernel, out_shape=jax.ShapeDtypeStruct(rows.shape, F...  18.8 us
    pallas_call x1, Pallas kernels, update(): pl.pallas_call(update_kernel, grid=(n_blocks,), out_shape=(jax.ShapeDtype...  16.9 us
    pallas_call x1, Pallas kernels, weights_of(): pl.pallas_call(counts_kernel, out_shape=jax.ShapeDtypeStruct((nodes, 1),...  13.1 us
    pallas_call x1, Pallas kernels, prep(): pl.pallas_call(lambda *refs: prep_kernel(local_rows, n_row, *refs), grid=...  10.1 us
    all_to_all x1, starting transfers between devices, body(): lax.all_to_all(rest.reshape(n, per, NB), ('row', 'col'), split_axis=0, co...  8.99 us
  transfers between devices with their start and end apart: 1, of which 1 were waited for; matrix products, arithmetic and copies ran while one was open for 1% of the time, Pallas kernels for 1%

profile of v2, /device:TPU:1, one launch (start us, length us, event | category | flops | bytes accessed | tf_op | source)
XLA Modules:
  0.0 221.7 jit_solution(13819760636411862320)
XLA Ops:
  0.6 1.5 copy.5.district_ref
  2.2 13.1 %counts.1.refs_2_ = f32[512,1]{1,0:T(8,128)} custom-call(s32[512,1]{1,0:T(8,128)} %copy.5.district_ref), custom_call_target="tpu_custom_call" | custom-call | tf_op jit(solution)/shard_map/counts/pallas_call | solution.py:75
  15.3 0.8 dynamic_slice.6
  16.1 0.0 copy-start
  16.1 2.2 copy-done
  18.3 0.0 copy-start.2
  18.3 0.9 copy-done.2
  19.2 10.1 %prep.1 = (f32[512,2048]{1,0:T(8,128)S(1)}, f32[512,2048]{1,0:T(8,128)S(1)}) custom-call(f32[512,2048]{1,0:T(8,128)S(1)} %copy-done, f32[512,2048]{1,0:T(8,128)S(1)} %copy-done, f32[512,1]{1,0:T(8,128)S(1)} %copy-done.2, s32[1,512]{1,0:T(1,128)S(1)} %bitcast.5), custom_call_target="tpu_custom_call" | custom-call | tf_op jit(solution)/shard_map/prep/pallas_call | solution.py:125
  29.3 66.5 %sum_gram.1.gram_ref = f32[512,2048]{1,0:T(8,128)S(1)} custom-call(f32[512,2048]{1,0:T(8,128)S(1)} %get-tuple-element.6.a_ref), custom_call_target="tpu_custom_call" | custom-call | tf_op jit(solution)/shard_map/sum_gram/pallas_call | solution.py:229
  95.8 23.7 %factor.1.inverse_ref = f32[512,512]{1,0:T(8,128)S(1)} custom-call(f32[512,2048]{1,0:T(8,128)S(1)} %sum_gram.1.gram_ref), custom_call_target="tpu_custom_call" | custom-call | tf_op jit(solution)/shard_map/factor/pallas_call | solution.py:311
  119.6 16.9 %update.1 = (f32[16,8,32,256]{3,2,1,0:T(8,128)S(1)}, f32[512,2048]{1,0:T(8,128)S(1)}) custom-call(f32[512,512]{1,0:T(8,128)S(1)} %factor.1.inverse_ref, f32[512,2048]{1,0:T(8,128)S(1)} %get-tuple-element.7.left_ref.rows_ref, f32[512,2048]{1,0:T(8,128)S(1)} %get-tuple-element.7.left_ref.rows_ref, f32[512,2048]{1,0:T(8,128)S(1)} %sum_gram.1.gram_ref), custom_call_target="tpu_custom_call" | custom-call | tf_op jit(solution)/shard_map/update/pallas_call | solution.py:344
  136.5 0.0 copy-start.1
  136.5 2.0 copy-done.1
  138.5 0.0 copy-start.4
  138.5 2.0 copy-done.4
  140.5 0.0 copy-start.5
  140.5 9.0 %all-to-all-start = ((f32[128,32,256]{2,1,0:T(8,128)}), f32[128,32,256]{2,1,0:T(8,128)}, u32[]{:S(2)}, u32[]{:S(2)}) async-start(f32[128,32,256]{2,1,0:T(8,128)} %bitcast.4), calls=%async_computation | async-start | bytes 8388608 | tf_op jit(solution)/shard_map/all_to_all | solution.py:445
  149.5 0.0 copy-done.5
  149.5 0.7 reshape.21.refs_0_
  150.3 2.7 %route.1.place_ref = s32[128,32]{1,0:T(8,128)} custom-call(s32[128,512]{1,0:T(8,128)} %reshape.21.refs_0_), custom_call_target="tpu_custom_call" | custom-call | tf_op jit(solution)/shard_map/route/pallas_call | solution.py:387
  153.0 1.9 constant_dynamic-slice_fusion
  154.9 47.3 %all-to-all-done = f32[128,32,256]{2,1,0:T(8,128)} async-done(((f32[128,32,256]{2,1,0:T(8,128)}), f32[128,32,256]{2,1,0:T(8,128)}, u32[]{:S(2)}, u32[]{:S(2)}) %all-to-all-start) | async-done | bytes 4194336 | tf_op jit(solution)/shard_map/all_to_all | solution.py:445
  202.1 0.0 copy-start.3
  202.1 0.8 copy-done.3
  203.0 18.8 %place.1 = f32[4096,256]{1,0:T(8,128)} custom-call(s32[128,32]{1,0:T(8,128)S(1)} %copy-done.3, f32[4096,256]{1,0:T(8,128)} %bitcast.3.rows_ref), custom_call_target="tpu_custom_call" | custom-call | tf_op jit(solution)/shard_map/place/pallas_call | solution.py:420
Async XLA Ops:
  16.1 2.2 copy-start
  18.3 0.9 copy-start.2
  136.5 2.0 copy-start.1
  138.5 2.0 copy-start.4
  140.5 9.0 %copy-start.5 = (s32[65536]{0:T(1024)S(1)}, s32[65536]{0:T(1024)}, u32[]{:S(2)}) copy-start(s32[65536]{0:T(1024)} %param.5) | copy-start | bytes 786436
  140.5 61.6 %all-to-all-start = ((f32[128,32,256]{2,1,0:T(8,128)}), f32[128,32,256]{2,1,0:T(8,128)}, u32[]{:S(2)}, u32[]{:S(2)}) async-start(f32[128,32,256]{2,1,0:T(8,128)} %bitcast.4), calls=%async_computation | async-start | bytes 8388608 | tf_op jit(solution)/shard_map/all_to_all | solution.py:445
  202.1 0.8 copy-start.3

commit v3 on v2

v3 whole, which is shorter than its diff:
```python
import jax
import jax.numpy as jnp
from jax import lax
from jax.experimental import pallas as pl
from jax.experimental.pallas import tpu as pltpu
from jax.sharding import PartitionSpec as P

MESH = pl.DeviceIdType.MESH
NB = 256
PANELS = 2
K = PANELS * NB
DIST_MEAN = 256
HIGH = lax.Precision.HIGHEST
F32 = jnp.float32
BF16 = jnp.bfloat16
VMEM = pl.BlockSpec(memory_space=pltpu.VMEM)


def split2(x):
    hi = x.astype(BF16)
    return hi, (x - hi.astype(F32)).astype(BF16)


def dims(a, b):
    return (((a,), (b,)), ((), ()))


def mm(x, y, a=1, b=0):
    return lax.dot_general(x, y, dims(a, b), preferred_element_type=F32)


def mm3(xh, xl, yh, yl, a=1, b=0):
    return mm(xh, yh, a, b) + (mm(xh, yl, a, b) + mm(xl, yh, a, b))


def counts_kernel(district_ref, weight_ref, own, got, send_sem, recv_sem):
    row, col = lax.axis_index("row"), lax.axis_index("col")
    n_row, n_col = lax.axis_size("row"), lax.axis_size("col")
    n = n_row * n_col
    me = row * n_col + col
    steps = (n - 2, n - 1, 1, 2)

    def peer(step):
        other = lax.rem(me + step, n)
        return other // n_col, lax.rem(other, n_col)

    barrier = pltpu.get_barrier_semaphore()
    for step in steps:
        pl.semaphore_signal(barrier, inc=1, device_id=peer(step), device_id_type=MESH)
    nodes = district_ref.shape[0]
    lanes = lax.broadcasted_iota(jnp.int32, (nodes, 256), 1)
    member = district_ref[...] == lanes
    hist = jnp.sum(jnp.where(member, 1.0, 0.0), axis=0, keepdims=True)
    own[...] = jnp.broadcast_to(hist, own.shape)
    pl.semaphore_wait(barrier, 4)
    copies = []
    for k, step in enumerate(steps):
        copy = pltpu.make_async_remote_copy(
            own, got.at[k], send_sem.at[k], recv_sem.at[k], device_id=peer(step), device_id_type=MESH
        )
        copy.start()
        copies.append(copy)
    for copy in copies:
        copy.wait()
    total = own[...]
    valid = (me + 2 < n, me + 1 < n, me >= 1, me >= 2)
    for k in range(4):
        total = total + got[k] * jnp.where(valid[k], 1.0, 0.0)
    scale = jnp.sqrt(DIST_MEAN / jnp.maximum(total, 1.0))[0:1, :]
    weight_ref[...] = jnp.sum(jnp.where(member, scale, 0.0), axis=1, keepdims=True)


def weights_of(district):
    nodes = district.shape[0]
    return pl.pallas_call(
        counts_kernel,
        out_shape=jax.ShapeDtypeStruct((nodes, 1), F32),
        in_specs=[VMEM],
        out_specs=VMEM,
        scratch_shapes=[
            pltpu.VMEM((8, 256), F32),
            pltpu.VMEM((4, 8, 256), F32),
            pltpu.SemaphoreType.DMA((4,)),
            pltpu.SemaphoreType.DMA((4,)),
        ],
        compiler_params=pltpu.CompilerParams(collective_id=0, has_side_effects=True),
        name="counts",
    )(district.reshape(nodes, 1))


def prep_kernel(local_rows, n_row, panel_ref, x_ref, weight_ref, target_ref, rows_ref, gram_ref, left_hi, left_lo, perm):
    nodes = x_ref.shape[0]
    per = nodes // n_row

    @pl.when(pl.program_id(0) == 0)
    def _():
        left = panel_ref[...] * weight_ref[...]
        hi, lo = split2(left)
        left_hi[...] = hi.T
        left_lo[...] = lo.T
        owner = target_ref[...] // local_rows
        groups = lax.broadcasted_iota(jnp.int32, (n_row, nodes), 0)
        mask = jnp.where(owner == groups, 1.0, 0.0)
        before = jnp.where(
            lax.broadcasted_iota(jnp.int32, (nodes, nodes), 0) < lax.broadcasted_iota(jnp.int32, (nodes, nodes), 1), 1.0, 0.0
        ).astype(BF16)
        rank = mm(mask.astype(BF16), before)
        base = groups.astype(F32) * per
        place = jnp.sum(mask * (rank + base), axis=0, keepdims=True).astype(jnp.int32)
        perm[...] = jnp.where(place == lax.broadcasted_iota(jnp.int32, (nodes, nodes), 0), 1.0, 0.0).astype(BF16)

    x = x_ref[...] * weight_ref[...]
    hi = x.astype(BF16)
    rest = x - hi.astype(F32)
    mid = rest.astype(BF16)
    low = (rest - mid.astype(F32)).astype(BF16)
    p = perm[...]
    rows_ref[...] = (mm(p, hi) + mm(p, mid)) + mm(p, low)
    gram_ref[...] = mm3(left_hi[...], left_lo[...], hi, mid)


def prep(snapshots, weight, mine, n_row, local_rows):
    nodes, snaps = snapshots.shape
    out = jax.ShapeDtypeStruct((nodes, snaps), F32), jax.ShapeDtypeStruct((K, snaps), F32)
    return pl.pallas_call(
        lambda *refs: prep_kernel(local_rows, n_row, *refs),
        grid=(snaps // NB,),
        out_shape=out,
        in_specs=[
            pl.BlockSpec((nodes, K), lambda i: (0, 0)),
            pl.BlockSpec((nodes, NB), lambda i: (0, i)),
            pl.BlockSpec((nodes, 1), lambda i: (0, 0)),
            pl.BlockSpec((1, nodes), lambda i: (0, 0)),
        ],
        out_specs=(pl.BlockSpec((nodes, NB), lambda i: (0, i)), pl.BlockSpec((K, NB), lambda i: (0, i))),
        scratch_shapes=[pltpu.VMEM((K, nodes), BF16), pltpu.VMEM((K, nodes), BF16), pltpu.VMEM((nodes, nodes), BF16)],
        compiler_params=pltpu.CompilerParams(vmem_limit_bytes=32 << 20),
        name="prep",
    )(snapshots, snapshots, weight, mine.reshape(1, nodes))


def hdot(x, y, a=1, b=0):
    return lax.dot_general(x, y, dims(a, b), precision=HIGH, preferred_element_type=F32)


def eliminate(work, top, start, halfway):
    b=128; groups=b//8
    sub=lax.broadcasted_iota(jnp.int32,(8,b),0); lane=lax.broadcasted_iota(jnp.int32,(8,b),1)
    x=[work[pl.ds(pl.multiple_of(start+8*g,8),8), pl.ds(start,b)] for g in range(groups)]
    for g0 in range(groups):
        if g0 == groups // 2:
            halfway()
        first=8*g0
        column=[[jnp.broadcast_to(x[g][:,first+c:first+c+1],(8,b)) for c in range(8)] for g in range(g0,groups)]
        inside=(lane>=first)&(lane<first+8)
        own=jnp.where(inside,jnp.where(lane-first==sub,1.0,0.0),x[g0])
        y=[jnp.broadcast_to(own[c:c+1,:],(8,b)) for c in range(8)]
        d=[[jnp.broadcast_to(column[0][k][c:c+1,:],(8,b)) for k in range(c+1)] for c in range(8)]
        inv=[]; low=[[None]*8 for _ in range(8)]
        for k in range(8):
            inv.append(1.0/d[k][k])
            for c in range(k+1,8):
                low[c][k]=d[c][k]*inv[k]
            for c in range(k+1,8):
                for m in range(k+1,c+1):
                    d[c][m]=d[c][m]-low[c][k]*d[m][k]
                y[c]=y[c]-low[c][k]*y[k]
        t=jnp.zeros((8,b),F32)
        for c in range(8):
            t=jnp.where(sub==c,y[c]*lax.rsqrt(d[c][c]),t)
        top[pl.ds(first,8),:]=jnp.where(lane<first+8,t,0.0)
        v=[None]*8
        for c in reversed(range(8)):
            a=y[c]*inv[c]
            for k in reversed(range(c+1,8)):
                a=a-low[k][c]*v[k]
            v[c]=a
        for g in range(g0+1,groups):
            m=column[g-g0]
            u=[m[c]*v[c] for c in range(8)]
            s=((u[0]+u[1])+(u[2]+u[3]))+((u[4]+u[5])+(u[6]+u[7]))
            x[g]=jnp.where(inside,0.0,x[g])-s
def main_kernel(local_rows, per, gram_ref, rows_ref, target_ref, coef_ref, out_ref,
                full, got_core, acc, got_panel, got1, got2, got3, work, top, upper, inverse,
                inv_hi, inv_lo, q_hi, q_lo, stage, arrived0, arrived1, hot_row, hot_lo, hot_hi, index, index_smem,
                core_send, core_recv, panel_send, panel_recv, rest_send, rest_recv, row_send, row_recv, local_sem):
    row, col = lax.axis_index("row"), lax.axis_index("col")
    n_row, n_col = lax.axis_size("row"), lax.axis_size("col")
    me = row * n_col + col
    y, x, z, core = row // 4, lax.rem(row, 4), col // 2, lax.rem(col, 2)
    half = K // 2
    sibling = (row, z * 2 + 1 - core)
    mine = core * half

    def ds(start, size):
        return pl.ds(pl.multiple_of(start, size), size)

    def remote(src, dst, send, recv, to):
        return pltpu.make_async_remote_copy(src, dst, send, recv, device_id=to, device_id_type=MESH)

    def row_at(r):
        return lax.rem(y + r // 4, 4) * 4 + lax.rem(x + lax.rem(r, 4), 4)

    barrier = pltpu.get_barrier_semaphore()

    def greet(t, carry):
        to = (row_at(lax.rem(t, 16)), lax.rem(col + t // 16, n_col))
        pl.semaphore_signal(barrier, inc=1, device_id=to, device_id_type=MESH)
        return carry

    lax.fori_loop(1, n_row * n_col, greet, 0)
    pl.semaphore_wait(barrier, n_row * n_col - 1)

    def chunk(q):
        return pl.ds(q * K, K)

    def core_copy(q):
        return remote(gram_ref.at[ds((1 - core) * half, half), chunk(q)], got_core.at[q], core_send.at[q], core_recv.at[q], sibling)

    def core_back(q):
        piece = full.at[ds(mine, half), chunk(q)]
        return remote(piece, piece, core_send.at[4 + q], core_recv.at[4 + q], sibling)

    def take_core(q):
        core_copy(q).wait()
        acc[q] = gram_ref[ds(mine, half), chunk(q)] + got_core[q]

    def panel_peer(t):
        t = lax.rem(t * 29, 64)
        return row_at(lax.rem(t, 16)), lax.rem(z + t // 16, 4)

    def panel_out(t):
        r, c = panel_peer(t)
        src = acc.at[0, ds(r * 16, 16), ds(c * 128, 128)]
        return remote(src, got_panel.at[t], panel_send.at[0, t], panel_recv.at[0, t], (r, c * 2 + core))

    def panel_back(t):
        r, c = panel_peer(t)
        piece = full.at[ds(mine + row * 16, 16), ds(z * 128, 128)]
        return remote(piece, piece, panel_send.at[1, t], panel_recv.at[1, t], (r, c * 2 + core))

    def loop(lo, hi, act):
        def step(t, carry):
            act(t)
            return carry

        lax.fori_loop(lo, hi, step, 0)

    core_copy(0).start()
    for q in (1, 2, 3):
        core_copy(q).start()
    take_core(0)
    loop(1, 64, lambda t: panel_out(t).start())
    total = acc[0, ds(row * 16, 16), ds(z * 128, 128)]

    def add(t, total):
        panel_out(t).wait()
        return total + got_panel[t]

    total = lax.fori_loop(1, 64, add, total)
    full[ds(mine + row * 16, 16), ds(z * 128, 128)] = total
    loop(1, 64, lambda t: panel_back(t).start())

    def place_of(q):
        first = lax.rem(q + core, 3)
        out = []
        for k in range(3):
            axis = lax.rem(first + k, 3)
            ex, ey, ez = [jnp.where(axis == v, 1, 0) for v in range(3)]
            at = ex * x + ey * y + ez * z

            def peer(d, ex=ex, ey=ey, ez=ez):
                px, py, pz = lax.rem(x + d * ex, 4), lax.rem(y + d * ey, 4), lax.rem(z + d * ez, 4)
                return py * 4 + px, pz * 2 + core

            out.append((at, peer))
        return out

    where = {q: place_of(q) for q in (1, 2, 3)}
    DIST = (1, 2, 3)

    def rest_copies(q, stage_):
        (p1, peer1), (p2, peer2), (p3, peer3) = where[q]
        q1, q2 = half // 4, half // 16
        at1 = p1 * q1
        at2 = at1 + p2 * q2
        copies = []
        for d in DIST:
            slot = stage_ * 3 + d - 1
            sems = rest_send.at[q - 1, slot], rest_recv.at[q - 1, slot]
            if stage_ == 0:
                src, dst, to = acc.at[q, ds(lax.rem(p1 + d, 4) * q1, q1), :], got1.at[q - 1, d - 1], peer1(d)
            elif stage_ == 1:
                src, dst, to = acc.at[q, ds(at1 + lax.rem(p2 + d, 4) * q2, q2), :], got2.at[q - 1, d - 1], peer2(d)
            elif stage_ == 2:
                src = acc.at[q, ds(at2, q2), ds(lax.rem(p3 + d, 4) * 128, 128)]
                dst, to = got3.at[q - 1, d - 1], peer3(d)
            elif stage_ == 3:
                src = dst = full.at[ds(mine + at2, q2), pl.ds(pl.multiple_of(q * K + p3 * 128, 128), 128)]
                to = peer3(d)
            elif stage_ == 4:
                src = dst = full.at[ds(mine + at2, q2), chunk(q)]
                to = peer2(d)
            else:
                src = dst = full.at[ds(mine + at1, q1), chunk(q)]
                to = peer1(d)
            copies.append(remote(src, dst, *sems, to))
        return copies

    def start_rest(stage_):
        for q in (1, 2, 3):
            for copy in rest_copies(q, stage_):
                copy.start()

    def end_rest(stage_):
        for q in (1, 2, 3):
            for copy in rest_copies(q, stage_):
                copy.wait()

    def rest_step(k):
        if k == 0:
            for q in (1, 2, 3):
                take_core(q)
            start_rest(0)
        elif k <= 6:
            end_rest(k - 1)
            q1, q2 = half // 4, half // 16
            for q in (1, 2, 3):
                (p1, _), (p2, _), (p3, _) = where[q]
                at1, at2 = p1 * q1, p1 * q1 + p2 * q2
                if k == 1:
                    acc[q, ds(at1, q1), :] = (acc[q, ds(at1, q1), :] + got1[q - 1, 0]) + (got1[q - 1, 1] + got1[q - 1, 2])
                elif k == 2:
                    acc[q, ds(at2, q2), :] = (acc[q, ds(at2, q2), :] + got2[q - 1, 0]) + (got2[q - 1, 1] + got2[q - 1, 2])
                elif k == 3:
                    last = acc[q, ds(at2, q2), ds(p3 * 128, 128)]
                    full[ds(mine + at2, q2), pl.ds(pl.multiple_of(q * K + p3 * 128, 128), 128)] = (last + got3[q - 1, 0]) + (
                        got3[q - 1, 1] + got3[q - 1, 2]
                    )
            if k < 6:
                start_rest(k)
            else:
                for q in (1, 2, 3):
                    core_back(q).start()
        else:
            for q in (1, 2, 3):
                core_back(q).wait()

    loop(1, 64, lambda t: panel_back(t).wait())
    core_back(0).start()
    rest_step(0)
    core_back(0).wait()

    b = 128
    blocks = K // b
    work[...] = full[:, 0:K]
    cols = lax.broadcasted_iota(jnp.int32, (b, K), 1)
    lines = lax.broadcasted_iota(jnp.int32, (b, K), 0)

    def block(k, carry):
        start = pl.multiple_of(k * b, b)

        def at(k0, step):
            @pl.when(k == k0)
            def _():
                rest_step(step)

        def halfway():
            at(0, 1)
            at(1, 3)
            at(2, 5)
            at(3, 6)

        eliminate(work, top, start, halfway)
        here = (cols >= start) & (cols < start + b)
        line = jnp.where(here, jnp.where(cols - start == lines, 1.0, 0.0), work[pl.ds(start, b), :])
        up = hdot(top[...], line)
        upper[...] = up
        inverse[pl.ds(start, b), :] = jnp.where(cols < start + b, up, 0.0)

        def below(i, c):
            to = pl.multiple_of(i * b, b)
            left = upper[:, pl.ds(to, b)]
            work[pl.ds(to, b), :] = jnp.where(here, 0.0, work[pl.ds(to, b), :]) - hdot(left, upper[...], 0, 0)
            return c

        lax.fori_loop(k + 1, blocks, below, 0)
        at(0, 2)
        at(1, 4)
        return carry

    lax.fori_loop(0, blocks, block, 0)
    hi, lo = split2(inverse[...])
    inv_hi[...], inv_lo[...] = hi, lo
    left_hi, left_lo = split2(rows_ref[:, 0:K])
    q_hi[...], q_lo[...] = split2(mm3(left_hi, left_lo, hi, lo, 1, 1))
    rest_step(7)

    lanes = NB // 2
    arrived = (arrived0, arrived1)

    def message(j, t, h):
        r = row_at(lax.rem(t + 5 * j, 16))
        src = stage.at[j, h, ds(r * per, per), :]
        dst = arrived[h].at[ds(me * per, per), :]
        slot = j * 16 + t
        return remote(src, dst, row_send.at[h, slot], row_recv.at[h, slot], (r, lax.rem(col + j, n_col)))

    def own(h):
        return pltpu.make_async_copy(stage.at[0, h, ds(row * per, per), :], arrived[h].at[ds(me * per, per), :], local_sem.at[h])

    def form(j, carry):
        c = lax.rem(col + j, n_col)
        at = pl.ds(pl.multiple_of(c * NB, NB), NB)
        g_hi, g_lo = split2(full[:, at])
        coef = mm3(inv_hi[...], inv_lo[...], g_hi, g_lo)

        @pl.when(j == 0)
        def _():
            coef_ref[...] = coef

        c_hi, c_lo = split2(coef)
        rest = rows_ref[:, at] - mm3(q_hi[...], q_lo[...], c_hi, c_lo)
        stage[j, 0] = rest[:, :lanes]
        stage[j, 1] = rest[:, lanes:]

        @pl.when(j == 0)
        def _():
            own(0).start()
            own(1).start()

        def release(i, carry):
            message(i, j - i + 1, 0).start()
            return carry

        lax.fori_loop(0, j + 1, release, 0)
        return carry

    lax.fori_loop(0, n_col, form, 0)

    def late(t, carry):
        def one(j, carry):
            @pl.when(lax.rem(t, 16) + j > 8)
            def _():
                message(j, lax.rem(t, 16), 0).start()

            return carry

        lax.fori_loop(0, n_col, one, 0)
        return carry

    lax.fori_loop(1, 16, late, 0)
    loop(1, n_col, lambda j: message(j, 0, 0).start())

    def second(t, carry):
        loop(0, n_col, lambda j: message(j, t, 1).start())
        return carry

    lax.fori_loop(1, 16, second, 0)
    loop(1, n_col, lambda j: message(j, 0, 1).start())

    target = target_ref[...]
    n, nodes = target.shape
    mask = jnp.where(target // local_rows == row, 1.0, 0.0)
    before = jnp.where(
        lax.broadcasted_iota(jnp.int32, (nodes, nodes), 0) < lax.broadcasted_iota(jnp.int32, (nodes, nodes), 1), 1.0, 0.0
    ).astype(BF16)
    rank = jnp.where(mask > 0.0, mm(mask.astype(BF16), before), -1.0)
    value = lax.rem(target, local_rows).astype(F32)
    wide = lax.broadcasted_iota(jnp.int32, (n, 128), 1)
    source = lax.broadcasted_iota(jnp.int32, (n, 128), 0)
    for k in range(per):
        spot = jnp.sum(jnp.where(rank == float(k), value, 0.0), axis=1, keepdims=True).astype(jnp.int32)
        number = source * per + k
        low = wide == lax.rem(spot, 128)
        hot_row[pl.ds(k * n, n), :] = jnp.where(wide == spot // 128, 1.0, 0.0).astype(BF16)
        hot_lo[pl.ds(k * n, n), :] = jnp.where(low, lax.rem(number, 64).astype(F32), 0.0).astype(BF16)
        hot_hi[pl.ds(k * n, n), :] = jnp.where(low, (number // 64).astype(F32), 0.0).astype(BF16)
    hot = hot_row[...]
    found = mm(hot, hot_lo[...], 0, 0) + 64.0 * mm(hot, hot_hi[...], 0, 0)
    index[...] = jnp.clip(found[: local_rows // 128, :].astype(jnp.int32), 0, n * per - 1)
    to_smem = pltpu.make_async_copy(index, index_smem, local_sem.at[2])
    to_smem.start()
    to_smem.wait()

    sub = lax.broadcasted_iota(jnp.int32, (8, lanes), 0)
    for h in range(2):
        own(h).wait()

        def arrive(t, carry):
            loop(jnp.where(t == 0, 1, 0), n_col, lambda j: message(j, t, h).wait())
            return carry

        lax.fori_loop(0, 16, arrive, 0)

        def gather(i, carry):
            for u in range(16):
                rows = jnp.broadcast_to(arrived[h][pl.ds(index_smem[i, u * 8], 1), :], (8, lanes))
                for k in range(1, 8):
                    one = jnp.broadcast_to(arrived[h][pl.ds(index_smem[i, u * 8 + k], 1), :], (8, lanes))
                    rows = jnp.where(sub == k, one, rows)
                out_ref[pl.ds(pl.multiple_of(i * 128 + u * 8, 8), 8), pl.ds(h * lanes, lanes)] = rows
            return carry

        lax.fori_loop(0, local_rows // 128, gather, 0)


def finish(gram, rows, target, n_row, n_col):
    nodes, snaps = rows.shape
    n = n_row * n_col
    local_rows = target.shape[0] // n_row
    per = nodes // n_row
    half = K // 2
    dma = pltpu.SemaphoreType.DMA
    return pl.pallas_call(
        lambda *refs: main_kernel(local_rows, per, *refs),
        out_shape=(jax.ShapeDtypeStruct((K, NB), F32), jax.ShapeDtypeStruct((local_rows, NB), F32)),
        in_specs=[VMEM] * 3,
        out_specs=(VMEM, VMEM),
        scratch_shapes=[
            pltpu.VMEM((K, snaps), F32),
            pltpu.VMEM((4, half, K), F32),
            pltpu.VMEM((4, half, K), F32),
            pltpu.VMEM((64, 16, 128), F32),
            pltpu.VMEM((3, 3, half // 4, K), F32),
            pltpu.VMEM((3, 3, half // 16, K), F32),
            pltpu.VMEM((3, 3, half // 16, 128), F32),
            pltpu.VMEM((K, K), F32),
            pltpu.VMEM((128, 128), F32),
            pltpu.VMEM((128, K), F32),
            pltpu.VMEM((K, K), F32),
            pltpu.VMEM((K, K), BF16),
            pltpu.VMEM((K, K), BF16),
            pltpu.VMEM((nodes, K), BF16),
            pltpu.VMEM((nodes, K), BF16),
            pltpu.VMEM((n_col, 2, nodes, NB // 2), F32),
            pltpu.VMEM((n * per, NB // 2), F32),
            pltpu.VMEM((n * per, NB // 2), F32),
            pltpu.VMEM((n * per, 128), BF16),
            pltpu.VMEM((n * per, 128), BF16),
            pltpu.VMEM((n * per, 128), BF16),
            pltpu.VMEM((local_rows // 128, 128), jnp.int32),
            pltpu.SMEM((local_rows // 128, 128), jnp.int32),
            dma((8,)),
            dma((8,)),
            dma((2, 64)),
            dma((2, 64)),
            dma((3, 18)),
            dma((3, 18)),
            dma((2, 128)),
            dma((2, 128)),
            dma((3,)),
        ],
        compiler_params=pltpu.CompilerParams(collective_id=1, has_side_effects=True, vmem_limit_bytes=56 << 20),
        name="finish",
    )(gram, rows, target.reshape(n, nodes))


def body(snapshots, district, target):
    n_row, n_col = lax.axis_size("row"), lax.axis_size("col")
    nodes_dev, snaps = snapshots.shape
    local_rows = target.shape[0] // n_row
    me = lax.axis_index(("row", "col"))
    mine = lax.dynamic_slice_in_dim(target, me * nodes_dev, nodes_dev)
    weight = weights_of(district)
    rows, gram = prep(snapshots, weight, mine, n_row, local_rows)
    return finish(gram, rows, target, n_row, n_col)


def solution(mesh):
    in_specs = (P(("row", "col"), None), P(("row", "col")), P())
    out_specs = (P(None, "col"), P("row", "col"))
    return jax.shard_map(body, mesh=mesh, in_specs=in_specs, out_specs=out_specs, check_vma=False)
```

time: 222 us -> 188 us (0.85)
  waiting for transfers between devices: 47.3 us -> 0 us
  Pallas kernels: 152 us -> 170 us
  starting transfers between devices: 8.99 us -> 0 us
  local copies, waits for them, and re-layouts: 12.9 us -> 17.4 us
    all_to_all x1 -> x0, waiting for transfers between devices: 47.3 us -> none  [body(): lax.all_to_all(rest.reshape(n, per, NB), ('row', 'col'), split_axis=0, co...]
    pallas_call x5 -> x1, Pallas kernels: 129 us -> 147 us  [finish(): pl.pallas_call(lambda *refs: main_kernel(local_rows, per, *refs), out_sha...]
    all_to_all x1 -> x0, starting transfers between devices: 8.99 us -> none  [body(): lax.all_to_all(rest.reshape(n, per, NB), ('row', 'col'), split_axis=0, co...]
    unnamed x12 -> x10, local copies, waits for them, and re-layouts: 7.96 us -> 13.4 us
  transfers between devices with their start and end apart: 1 -> 0, of which waited for: 1 -> 0; matrix products, arithmetic and copies ran while one was open for 1% -> 0% of each run, Pallas kernels for 1% -> 0%
where the time goes in v3:
time: 188 us
  Pallas kernels  170 us (90%)
  local copies, waits for them, and re-layouts  17.4 us (9%)
    pallas_call x1, Pallas kernels, finish(): pl.pallas_call(lambda *refs: main_kernel(local_rows, per, *refs), out_sha...  147 us
    unnamed x10, local copies, waits for them, and re-layouts  13.4 us
    pallas_call x1, Pallas kernels, weights_of(): pl.pallas_call(counts_kernel, out_shape=jax.ShapeDtypeStruct((nodes, 1),...  13.1 us
    pallas_call x1, Pallas kernels, prep(): pl.pallas_call(lambda *refs: prep_kernel(local_rows, n_row, *refs), grid=...  10.1 us

profile of v3, /device:TPU:1, one launch (start us, length us, event | category | flops | bytes accessed | tf_op | source)
XLA Modules:
  0.0 188.0 jit_solution(10911465413773719085)
XLA Ops:
  0.6 0.8 dynamic_slice.3
  1.4 1.5 copy.5.district_ref
  2.9 13.1 %counts.1.refs_2_ = f32[512,1]{1,0:T(8,128)} custom-call(s32[512,1]{1,0:T(8,128)} %copy.5.district_ref), custom_call_target="tpu_custom_call" | custom-call | tf_op jit(solution)/shard_map/counts/pallas_call | solution.py:75
  16.1 1.7 reshape.15.refs_2_
  17.8 0.0 copy-start
  17.8 2.2 %copy-done = f32[512,2048]{1,0:T(8,128)S(1)} copy-done((f32[512,2048]{1,0:T(8,128)S(1)}, f32[512,2048]{1,0:T(8,128)}, u32[]{:S(2)}) %copy-start) | copy-done | bytes 4194328
  20.0 0.0 copy-start.3
  20.0 0.9 copy-done.3
  20.9 10.1 %prep.1 = (f32[512,2048]{1,0:T(8,128)S(1)}, f32[512,2048]{1,0:T(8,128)S(1)}) custom-call(f32[512,2048]{1,0:T(8,128)S(1)} %copy-done, f32[512,2048]{1,0:T(8,128)S(1)} %copy-done, f32[512,1]{1,0:T(8,128)S(1)} %copy-done.3, s32[1,512]{1,0:T(1,128)S(1)} %bitcast.2), custom_call_target="tpu_custom_call" | custom-call | tf_op jit(solution)/shard_map/prep/pallas_call | solution.py:125
  31.0 0.0 copy-start.1
  31.0 1.9 %copy-done.1 = f32[512,2048]{1,0:T(8,128)} copy-done((f32[512,2048]{1,0:T(8,128)}, f32[512,2048]{1,0:T(8,128)S(1)}, u32[]{:S(2)}) %copy-start.1) | copy-done | bytes 4194328
  33.0 0.0 copy-start.2
  33.0 2.0 %copy-done.2 = f32[512,2048]{1,0:T(8,128)} copy-done((f32[512,2048]{1,0:T(8,128)}, f32[512,2048]{1,0:T(8,128)S(1)}, u32[]{:S(2)}) %copy-start.2) | copy-done | bytes 4194328
  35.0 146.6 %finish.1 = (f32[512,256]{1,0:T(8,128)}, f32[4096,256]{1,0:T(8,128)}) custom-call(f32[512,2048]{1,0:T(8,128)} %copy-done.2, f32[512,2048]{1,0:T(8,128)} %copy-done.1, s32[128,512]{1,0:T(8,128)} %reshape.15.refs_2_), custom_call_target="tpu_custom_call" | custom-call | tf_op jit(solution)/shard_map/finish/pallas_call | solution.py:515
  181.6 1.9 copy.8
  183.5 4.5 %copy.9 = f32[4096,256]{1,0:T(8,128)} copy(f32[4096,256]{1,0:T(8,128)} %get-tuple-element.9) | data formatting | bytes 8388608
Async XLA Ops:
  17.8 2.2 %copy-start = (f32[512,2048]{1,0:T(8,128)S(1)}, f32[512,2048]{1,0:T(8,128)}, u32[]{:S(2)}) copy-start(f32[512,2048]{1,0:T(8,128)} %refs_1_.1) | copy-start | bytes 12582916
  20.0 0.9 copy-start.3
  31.0 1.9 %copy-start.1 = (f32[512,2048]{1,0:T(8,128)}, f32[512,2048]{1,0:T(8,128)S(1)}, u32[]{:S(2)}) copy-start(f32[512,2048]{1,0:T(8,128)S(1)} %get-tuple-element.5.refs_1_) | copy-start | bytes 12582916
  33.0 2.0 %copy-start.2 = (f32[512,2048]{1,0:T(8,128)}, f32[512,2048]{1,0:T(8,128)S(1)}, u32[]{:S(2)}) copy-start(f32[512,2048]{1,0:T(8,128)S(1)} %get-tuple-element.4.refs_0_) | copy-start | bytes 12582916

commit v4 on v3

--- a/solution.py
+++ b/solution.py
@@ -86,57 +86,6 @@
         compiler_params=pltpu.CompilerParams(collective_id=0, has_side_effects=True),
         name="counts",
     )(district.reshape(nodes, 1))
-
-
-def prep_kernel(local_rows, n_row, panel_ref, x_ref, weight_ref, target_ref, rows_ref, gram_ref, left_hi, left_lo, perm):
-    nodes = x_ref.shape[0]
-    per = nodes // n_row
-
-    @pl.when(pl.program_id(0) == 0)
-    def _():
-        left = panel_ref[...] * weight_ref[...]
-        hi, lo = split2(left)
-        left_hi[...] = hi.T
-        left_lo[...] = lo.T
-        owner = target_ref[...] // local_rows
-        groups = lax.broadcasted_iota(jnp.int32, (n_row, nodes), 0)
-        mask = jnp.where(owner == groups, 1.0, 0.0)
-        before = jnp.where(
-            lax.broadcasted_iota(jnp.int32, (nodes, nodes), 0) < lax.broadcasted_iota(jnp.int32, (nodes, nodes), 1), 1.0, 0.0
-        ).astype(BF16)
-        rank = mm(mask.astype(BF16), before)
-        base = groups.astype(F32) * per
-        place = jnp.sum(mask * (rank + base), axis=0, keepdims=True).astype(jnp.int32)
-        perm[...] = jnp.where(place == lax.broadcasted_iota(jnp.int32, (nodes, nodes), 0), 1.0, 0.0).astype(BF16)
-
-    x = x_ref[...] * weight_ref[...]
-    hi = x.astype(BF16)
-    rest = x - hi.astype(F32)
-    mid = rest.astype(BF16)
-    low = (rest - mid.astype(F32)).astype(BF16)
-    p = perm[...]
-    rows_ref[...] = (mm(p, hi) + mm(p, mid)) + mm(p, low)
-    gram_ref[...] = mm3(left_hi[...], left_lo[...], hi, mid)
-
-
-def prep(snapshots, weight, mine, n_row, local_rows):
-    nodes, snaps = snapshots.shape
-    out = jax.ShapeDtypeStruct((nodes, snaps), F32), jax.ShapeDtypeStruct((K, snaps), F32)
-    return pl.pallas_call(
-        lambda *refs: prep_kernel(local_rows, n_row, *refs),
-        grid=(snaps // NB,),
-        out_shape=out,
-        in_specs=[
-            pl.BlockSpec((nodes, K), lambda i: (0, 0)),
-            pl.BlockSpec((nodes, NB), lambda i: (0, i)),
-            pl.BlockSpec((nodes, 1), lambda i: (0, 0)),
-            pl.BlockSpec((1, nodes), lambda i: (0, 0)),
-        ],
-        out_specs=(pl.BlockSpec((nodes, NB), lambda i: (0, i)), pl.BlockSpec((K, NB), lambda i: (0, i))),
-        scratch_shapes=[pltpu.VMEM((K, nodes), BF16), pltpu.VMEM((K, nodes), BF16), pltpu.VMEM((nodes, nodes), BF16)],
-        compiler_params=pltpu.CompilerParams(vmem_limit_bytes=32 << 20),
-        name="prep",
-    )(snapshots, snapshots, weight, mine.reshape(1, nodes))
 
 
 def hdot(x, y, a=1, b=0):
@@ -180,8 +129,8 @@
             u=[m[c]*v[c] for c in range(8)]
             s=((u[0]+u[1])+(u[2]+u[3]))+((u[4]+u[5])+(u[6]+u[7]))
             x[g]=jnp.where(inside,0.0,x[g])-s
-def main_kernel(local_rows, per, gram_ref, rows_ref, target_ref, coef_ref, out_ref,
-                full, got_core, acc, got_panel, got1, got2, got3, work, top, upper, inverse,
+def main_kernel(local_rows, per, x_ref, weight_ref, mine_ref, target_ref, coef_ref, out_ref,
+                rows_ref, gram_ref, left_hi, left_lo, perm, full, got_core, acc, got_panel, got1, got2, got3, work, top, upper, inverse,
                 inv_hi, inv_lo, q_hi, q_lo, stage, arrived0, arrived1, hot_row, hot_lo, hot_hi, index, index_smem,
                 core_send, core_recv, panel_send, panel_recv, rest_send, rest_recv, row_send, row_recv, local_sem):
     row, col = lax.axis_index("row"), lax.axis_index("col")
@@ -209,6 +158,34 @@
         return carry
 
     lax.fori_loop(1, n_row * n_col, greet, 0)
+    count = x_ref.shape[0]
+    weight = jnp.broadcast_to(weight_ref[...], (count, NB))
+    for k in range(PANELS):
+        hi, lo = split2(x_ref[:, k * NB : (k + 1) * NB] * weight)
+        left_hi[k * NB : (k + 1) * NB, :] = hi.T
+        left_lo[k * NB : (k + 1) * NB, :] = lo.T
+    groups = lax.broadcasted_iota(jnp.int32, (n_row, count), 0)
+    belongs = jnp.where(mine_ref[...] // local_rows == groups, 1.0, 0.0)
+    sooner = jnp.where(
+        lax.broadcasted_iota(jnp.int32, (count, count), 0) < lax.broadcasted_iota(jnp.int32, (count, count), 1), 1.0, 0.0
+    ).astype(BF16)
+    spot = mm(belongs.astype(BF16), sooner) + (groups * per).astype(F32)
+    spot = jnp.sum(belongs * spot, axis=0, keepdims=True).astype(jnp.int32)
+    perm[...] = jnp.where(spot == lax.broadcasted_iota(jnp.int32, (count, count), 0), 1.0, 0.0).astype(BF16)
+
+    def share(i, carry):
+        at = pl.ds(pl.multiple_of(i * NB, NB), NB)
+        v = x_ref[:, at] * weight
+        hi = v.astype(BF16)
+        rest = v - hi.astype(F32)
+        mid = rest.astype(BF16)
+        low = (rest - mid.astype(F32)).astype(BF16)
+        p = perm[...]
+        rows_ref[:, at] = (mm(p, hi) + mm(p, mid)) + mm(p, low)
+        gram_ref[:, at] = mm3(left_hi[...], left_lo[...], hi, mid)
+        return carry
+
+    lax.fori_loop(0, x_ref.shape[1] // NB, share, 0)
     pl.semaphore_wait(barrier, n_row * n_col - 1)
 
     def chunk(q):
@@ -505,8 +482,8 @@
         lax.fori_loop(0, local_rows // 128, gather, 0)
 
 
-def finish(gram, rows, target, n_row, n_col):
-    nodes, snaps = rows.shape
+def finish(snapshots, weight, mine, target, n_row, n_col):
+    nodes, snaps = snapshots.shape
     n = n_row * n_col
     local_rows = target.shape[0] // n_row
     per = nodes // n_row
@@ -515,9 +492,14 @@
     return pl.pallas_call(
         lambda *refs: main_kernel(local_rows, per, *refs),
         out_shape=(jax.ShapeDtypeStruct((K, NB), F32), jax.ShapeDtypeStruct((local_rows, NB), F32)),
-        in_specs=[VMEM] * 3,
+        in_specs=[VMEM] * 4,
         out_specs=(VMEM, VMEM),
         scratch_shapes=[
+            pltpu.VMEM((nodes, snaps), F32),
+            pltpu.VMEM((K, snaps), F32),
+            pltpu.VMEM((K, nodes), BF16),
+            pltpu.VMEM((K, nodes), BF16),
+            pltpu.VMEM((nodes, nodes), BF16),
             pltpu.VMEM((K, snaps), F32),
             pltpu.VMEM((4, half, K), F32),
             pltpu.VMEM((4, half, K), F32),
@@ -551,20 +533,18 @@
             dma((2, 128)),
             dma((3,)),
         ],
-        compiler_params=pltpu.CompilerParams(collective_id=1, has_side_effects=True, vmem_limit_bytes=56 << 20),
+        compiler_params=pltpu.CompilerParams(collective_id=1, has_side_effects=True, vmem_limit_bytes=46 << 20),
         name="finish",
-    )(gram, rows, target.reshape(n, nodes))
+    )(snapshots, weight, mine.reshape(1, nodes), target.reshape(n, nodes))
 
 
 def body(snapshots, district, target):
     n_row, n_col = lax.axis_size("row"), lax.axis_size("col")
     nodes_dev, snaps = snapshots.shape
-    local_rows = target.shape[0] // n_row
     me = lax.axis_index(("row", "col"))
     mine = lax.dynamic_slice_in_dim(target, me * nodes_dev, nodes_dev)
     weight = weights_of(district)
-    rows, gram = prep(snapshots, weight, mine, n_row, local_rows)
-    return finish(gram, rows, target, n_row, n_col)
+    return finish(snapshots, weight, mine, target, n_row, n_col)
 
 
 def solution(mesh):

time: 188 us -> 169 us (0.90)
  local copies, waits for them, and re-layouts: 17.4 us -> 7.05 us
  Pallas kernels: 170 us -> 161 us
    pallas_call x1 -> x0, Pallas kernels: 10.1 us -> none  [prep(): pl.pallas_call(lambda *refs: prep_kernel(local_rows, n_row, *refs), grid=...]
    unnamed x10 -> x4, local copies, waits for them, and re-layouts: 13.4 us -> 3.75 us
where the time goes in v4:
time: 169 us
  Pallas kernels  161 us (95%)
  local copies, waits for them, and re-layouts  7.05 us (4%)
    pallas_call x1, Pallas kernels, finish(): pl.pallas_call(lambda *refs: main_kernel(local_rows, per, *refs), out_sha...  148 us
    pallas_call x1, Pallas kernels, weights_of(): pl.pallas_call(counts_kernel, out_shape=jax.ShapeDtypeStruct((nodes, 1),...  13.1 us
    unnamed x4, local copies, waits for them, and re-layouts  3.75 us

profile of v4, /device:TPU:1, one launch (start us, length us, event | category | flops | bytes accessed | tf_op | source)
XLA Modules:
  0.0 169.1 jit_solution(1267161667291915751)
XLA Ops:
  0.6 0.8 dynamic_slice.3
  1.4 1.5 copy.5.district_ref
  2.9 13.1 %counts.1.refs_1_ = f32[512,1]{1,0:T(8,128)} custom-call(s32[512,1]{1,0:T(8,128)} %copy.5.district_ref), custom_call_target="tpu_custom_call" | custom-call | tf_op jit(solution)/shard_map/counts/pallas_call | solution.py:75
  16.1 1.0 reshape.15.refs_3_
  17.1 0.0 copy-start
  17.1 0.9 copy-done
  18.0 148.2 %finish.1 = (f32[512,256]{1,0:T(8,128)S(1)}, f32[4096,256]{1,0:T(8,128)S(1)}) custom-call(f32[512,2048]{1,0:T(8,128)} %refs_0_.1, f32[512,1]{1,0:T(8,128)S(1)} %copy-done, s32[1,512]{1,0:T(1,128)S(1)} %bitcast.2, s32[128,512]{1,0:T(8,128)S(1)} %reshape.15.refs_3_), custom_call_target="tpu_custom_call" | custom-call | tf_op jit(solution)/shard_map/finish/pallas_call | solution.py:492
  166.2 0.8 copy.8
  167.0 2.0 %copy.9 = f32[4096,256]{1,0:T(8,128)} copy(f32[4096,256]{1,0:T(8,128)S(1)} %get-tuple-element.5) | data formatting | bytes 8388608
Async XLA Ops:
  17.1 1.0 copy-start

commit v5 on v4

--- a/solution.py
+++ b/solution.py
@@ -224,10 +224,10 @@
         lax.fori_loop(lo, hi, step, 0)
 
     core_copy(0).start()
+    take_core(0)
+    loop(1, 64, lambda t: panel_out(t).start())
     for q in (1, 2, 3):
         core_copy(q).start()
-    take_core(0)
-    loop(1, 64, lambda t: panel_out(t).start())
     total = acc[0, ds(row * 16, 16), ds(z * 128, 128)]
 
     def add(t, total):
@@ -390,7 +390,13 @@
         c = lax.rem(col + j, n_col)
         at = pl.ds(pl.multiple_of(c * NB, NB), NB)
         g_hi, g_lo = split2(full[:, at])
-        coef = mm3(inv_hi[...], inv_lo[...], g_hi, g_lo)
+        coef = jnp.concatenate(
+            [
+                mm3(inv_hi[:NB, :NB], inv_lo[:NB, :NB], g_hi[:NB], g_lo[:NB]),
+                mm3(inv_hi[NB:, :], inv_lo[NB:, :], g_hi, g_lo),
+            ],
+            axis=0,
+        )
 
         @pl.when(j == 0)
         def _():
@@ -407,7 +413,13 @@
             own(1).start()
 
         def release(i, carry):
-            message(i, j - i + 1, 0).start()
+            t = 2 * (j - i) + 1
+            message(i, t, 0).start()
+
+            @pl.when(t < 15)
+            def _():
+                message(i, t + 1, 0).start()
+
             return carry
 
         lax.fori_loop(0, j + 1, release, 0)
@@ -417,9 +429,9 @@
 
     def late(t, carry):
         def one(j, carry):
-            @pl.when(lax.rem(t, 16) + j > 8)
+            @pl.when(t + 2 * j > 16)
             def _():
-                message(j, lax.rem(t, 16), 0).start()
+                message(j, t, 0).start()
 
             return carry
 

time: 169 us -> 165 us (0.976)
  Pallas kernels: 161 us -> 157 us
    pallas_call x1, Pallas kernels: 148 us -> 144 us  [finish(): pl.pallas_call(lambda *refs: main_kernel(local_rows, per, *refs), out_sha...]
where the time goes in v5:
time: 165 us; the launch traced here: 164 us
  Pallas kernels  157 us (95%)
  local copies, waits for them, and re-layouts  7.05 us (4%)
    pallas_call x1, Pallas kernels, finish(): pl.pallas_call(lambda *refs: main_kernel(local_rows, per, *refs), out_sha...  144 us
    pallas_call x1, Pallas kernels, weights_of(): pl.pallas_call(counts_kernel, out_shape=jax.ShapeDtypeStruct((nodes, 1),...  13.1 us
    unnamed x4, local copies, waits for them, and re-layouts  3.75 us

profile of v5, /device:TPU:1, one launch (start us, length us, event | category | flops | bytes accessed | tf_op | source)
XLA Modules:
  0.0 164.4 jit_solution(10247229913585361782)
XLA Ops:
  0.6 0.8 dynamic_slice.3
  1.4 1.5 copy.5.district_ref
  2.9 13.1 %counts.1.refs_1_ = f32[512,1]{1,0:T(8,128)} custom-call(s32[512,1]{1,0:T(8,128)} %copy.5.district_ref), custom_call_target="tpu_custom_call" | custom-call | tf_op jit(solution)/shard_map/counts/pallas_call | solution.py:75
  16.1 1.0 reshape.15.refs_3_
  17.1 0.0 copy-start
  17.1 0.9 copy-done
  18.0 143.6 %finish.1 = (f32[512,256]{1,0:T(8,128)S(1)}, f32[4096,256]{1,0:T(8,128)S(1)}) custom-call(f32[512,2048]{1,0:T(8,128)} %refs_0_.1, f32[512,1]{1,0:T(8,128)S(1)} %copy-done, s32[1,512]{1,0:T(1,128)S(1)} %bitcast.2, s32[128,512]{1,0:T(8,128)S(1)} %reshape.15.refs_3_), custom_call_target="tpu_custom_call" | custom-call | tf_op jit(solution)/shard_map/finish/pallas_call | solution.py:504
  161.6 0.8 copy.8
  162.4 2.0 %copy.9 = f32[4096,256]{1,0:T(8,128)} copy(f32[4096,256]{1,0:T(8,128)S(1)} %get-tuple-element.5) | data formatting | bytes 8388608
Async XLA Ops:
  17.1 1.0 copy-start

commit v6 on v5

--- a/solution.py
+++ b/solution.py
@@ -129,8 +129,8 @@
             u=[m[c]*v[c] for c in range(8)]
             s=((u[0]+u[1])+(u[2]+u[3]))+((u[4]+u[5])+(u[6]+u[7]))
             x[g]=jnp.where(inside,0.0,x[g])-s
-def main_kernel(local_rows, per, x_ref, weight_ref, mine_ref, target_ref, coef_ref, out_ref,
-                rows_ref, gram_ref, left_hi, left_lo, perm, full, got_core, acc, got_panel, got1, got2, got3, work, top, upper, inverse,
+def main_kernel(local_rows, per, x_hbm, weight_ref, target_ref, coef_ref, out_ref,
+                x_ref, rows_ref, gram_ref, left_hi, left_lo, perm, full, got_core, acc, got_panel, got1, got2, got3, work, top, upper, inverse,
                 inv_hi, inv_lo, q_hi, q_lo, stage, arrived0, arrived1, hot_row, hot_lo, hot_hi, index, index_smem,
                 core_send, core_recv, panel_send, panel_recv, rest_send, rest_recv, row_send, row_recv, local_sem):
     row, col = lax.axis_index("row"), lax.axis_index("col")
@@ -150,6 +150,9 @@
     def row_at(r):
         return lax.rem(y + r // 4, 4) * 4 + lax.rem(x + lax.rem(r, 4), 4)
 
+    bring = pltpu.make_async_copy(x_hbm, x_ref, local_sem.at[3])
+    bring.start()
+
     barrier = pltpu.get_barrier_semaphore()
 
     def greet(t, carry):
@@ -158,6 +161,7 @@
         return carry
 
     lax.fori_loop(1, n_row * n_col, greet, 0)
+    bring.wait()
     count = x_ref.shape[0]
     weight = jnp.broadcast_to(weight_ref[...], (count, NB))
     for k in range(PANELS):
@@ -165,7 +169,7 @@
         left_hi[k * NB : (k + 1) * NB, :] = hi.T
         left_lo[k * NB : (k + 1) * NB, :] = lo.T
     groups = lax.broadcasted_iota(jnp.int32, (n_row, count), 0)
-    belongs = jnp.where(mine_ref[...] // local_rows == groups, 1.0, 0.0)
+    belongs = jnp.where(target_ref[pl.ds(me, 1), :] // local_rows == groups, 1.0, 0.0)
     sooner = jnp.where(
         lax.broadcasted_iota(jnp.int32, (count, count), 0) < lax.broadcasted_iota(jnp.int32, (count, count), 1), 1.0, 0.0
     ).astype(BF16)
@@ -413,12 +417,12 @@
             own(1).start()
 
         def release(i, carry):
-            t = 2 * (j - i) + 1
-            message(i, t, 0).start()
-
-            @pl.when(t < 15)
-            def _():
-                message(i, t + 1, 0).start()
+            for u in range(4):
+                t = 4 * (j - i) + 1 + u
+
+                @pl.when(t < 16)
+                def _(t=t):
+                    message(i, t, 0).start()
 
             return carry
 
@@ -429,7 +433,7 @@
 
     def late(t, carry):
         def one(j, carry):
-            @pl.when(t + 2 * j > 16)
+            @pl.when(t + 4 * j > 32)
             def _():
                 message(j, t, 0).start()
 
@@ -494,7 +498,7 @@
         lax.fori_loop(0, local_rows // 128, gather, 0)
 
 
-def finish(snapshots, weight, mine, target, n_row, n_col):
+def finish(snapshots, weight, target, n_row, n_col):
     nodes, snaps = snapshots.shape
     n = n_row * n_col
     local_rows = target.shape[0] // n_row
@@ -504,9 +508,10 @@
     return pl.pallas_call(
         lambda *refs: main_kernel(local_rows, per, *refs),
         out_shape=(jax.ShapeDtypeStruct((K, NB), F32), jax.ShapeDtypeStruct((local_rows, NB), F32)),
-        in_specs=[VMEM] * 4,
+        in_specs=[pl.BlockSpec(memory_space=pl.ANY), VMEM, VMEM],
         out_specs=(VMEM, VMEM),
         scratch_shapes=[
+            pltpu.VMEM((nodes, snaps), F32),
             pltpu.VMEM((nodes, snaps), F32),
             pltpu.VMEM((K, snaps), F32),
             pltpu.VMEM((K, nodes), BF16),
@@ -543,20 +548,17 @@
             dma((3, 18)),
             dma((2, 128)),
             dma((2, 128)),
-            dma((3,)),
+            dma((4,)),
         ],
         compiler_params=pltpu.CompilerParams(collective_id=1, has_side_effects=True, vmem_limit_bytes=46 << 20),
         name="finish",
-    )(snapshots, weight, mine.reshape(1, nodes), target.reshape(n, nodes))
+    )(snapshots, weight, target.reshape(n, nodes))
 
 
 def body(snapshots, district, target):
     n_row, n_col = lax.axis_size("row"), lax.axis_size("col")
-    nodes_dev, snaps = snapshots.shape
-    me = lax.axis_index(("row", "col"))
-    mine = lax.dynamic_slice_in_dim(target, me * nodes_dev, nodes_dev)
     weight = weights_of(district)
-    return finish(snapshots, weight, mine, target, n_row, n_col)
+    return finish(snapshots, weight, target, n_row, n_col)
 
 
 def solution(mesh):

time: 165 us -> 162 us (0.982)
  Pallas kernels: 157 us -> 155 us
    pallas_call x1, Pallas kernels: 144 us -> 142 us  [finish(): pl.pallas_call(lambda *refs: main_kernel(local_rows, per, *refs), out_sha...]
where the time goes in v6:
time: 162 us
  Pallas kernels  155 us (96%)
  local copies, waits for them, and re-layouts  6.28 us (4%)
    pallas_call x1, Pallas kernels, finish(): pl.pallas_call(lambda *refs: main_kernel(local_rows, per, *refs), out_sha...  142 us
    pallas_call x1, Pallas kernels, weights_of(): pl.pallas_call(counts_kernel, out_shape=jax.ShapeDtypeStruct((nodes, 1),...  13.1 us
    unnamed x4, local copies, waits for them, and re-layouts  3.75 us

profile of v6, /device:TPU:1, one launch (start us, length us, event | category | flops | bytes accessed | tf_op | source)
XLA Modules:
  0.0 161.7 jit_solution(12754179410299023268)
XLA Ops:
  0.6 1.5 copy.5.district_ref
  2.2 13.1 %counts.1.refs_1_ = f32[512,1]{1,0:T(8,128)} custom-call(s32[512,1]{1,0:T(8,128)} %copy.5.district_ref), custom_call_target="tpu_custom_call" | custom-call | tf_op jit(solution)/shard_map/counts/pallas_call | solution.py:75
  15.3 1.0 reshape.11.refs_2_
  16.3 0.0 copy-start
  16.3 0.9 copy-done
  17.2 141.6 %finish.1 = (f32[512,256]{1,0:T(8,128)S(1)}, f32[4096,256]{1,0:T(8,128)S(1)}) custom-call(f32[512,2048]{1,0:T(8,128)} %refs_0_.1, f32[512,1]{1,0:T(8,128)S(1)} %copy-done, s32[128,512]{1,0:T(8,128)S(1)} %reshape.11.refs_2_), custom_call_target="tpu_custom_call" | custom-call | tf_op jit(solution)/shard_map/finish/pallas_call | solution.py:508
  158.9 0.8 copy.8
  159.7 2.0 %copy.9 = f32[4096,256]{1,0:T(8,128)} copy(f32[4096,256]{1,0:T(8,128)S(1)} %get-tuple-element.5) | data formatting | bytes 8388608
Async XLA Ops:
  16.3 1.0 copy-start
